TPU v7x, 128 devices: a whole 4x4x4 slice. The times are simulated.
128 devices in a mesh: seq: 8 (over z, core), exp: 16 (over x, y).
Axes of the slice: x: 4, y: 4, z: 4, core: 2. Of those that a mesh axis runs over, the one named last changes fastest.
Arguments:
- residual: bfloat16 [16384, 8192], P(('seq', 'exp')), may hold values from -6 to 6
- expert_rows: bfloat16 [8, 16, 16, 24, 8192], P('seq', 'exp'), may hold values from -6 to 6
- expert_ids: int32 [16384, 2], P(('seq', 'exp')), may hold values from 0 to 15, as said below
- expert_slots: int32 [16384, 2], P(('seq', 'exp')), may hold values from 0 to 23, as said below
- combine_weights: float32 [16384, 2], P(('seq', 'exp')), may hold values from 0.1 to 0.9
- norm_gain: float32 [8192], replicated, may hold values from 0.1 to 1.9
- in_weight: bfloat16 [8192, 8192], P(None, 'exp'), may hold values from -0.0625 to 0.0625
- conv_weight: float32 [4, 8192], P(None, 'exp'), may hold values from -3 to 3
- conv_bias: float32 [8192], P('exp'), may hold values from -0.5 to 0.5
- bc_weight: bfloat16 [8192, 128], P('exp'), may hold values from -0.00390625 to 0.00390625
- dt_weight: bfloat16 [8192, 128], P('exp'), may hold values from -0.0625 to 0.0625
- dt_bias: float32 [128], P('exp'), may hold values from -2 to 0.5
- decay_log: float32 [128], P('exp'), may hold values from -14 to -3.2
- skip_gain: float32 [128], P('exp'), may hold values from -1 to 3
Outputs:
- scan_output: bfloat16 [16384, 8192], P('seq', 'exp')
Inputs may be any that keep to these rules, and one draw needn't show every extreme that they name: `expert_ids`: A token's two ids differ. The tokens of one device name no expert more than 24 times, and in each span one expert is named exactly 24 times by the tokens of every device of the span. `expert_slots`: A token's slot at its k-th expert counts the earlier (token, k) pairs of the same device, in row-major order, that name the same expert.
All inputs are finite; a program needn't handle non-finite values.
Results may differ from a plain program's by a relative error of at most 0.0074.
Values may be sent and summed in bfloat16 or wider, within the bound.
No kernel may reach another device: no remote copies, remote signals or barrier semaphores. Data moves between devices by JAX's collectives and lax.ppermute only.
A program may use at most 320 MiB of HBM per device.

v0:
```python
import jax
import jax.numpy as jnp
from jax import lax
from jax.sharding import PartitionSpec as P

TOPK = 2
KCONV = 4
HEAD = 64
NSTATE = 64
STRETCH = 256


def passed_along(value, axis, steps):
    count = lax.axis_size(axis)
    leading, last = (max(0, -steps), min(count, count - steps))
    return lax.ppermute(value, axis, [(source, source + steps) for source in range(leading, last)])


def block_terms(b_rows, c_rows, steps_dt, decays, values):
    running = jnp.cumsum(decays, axis=0)
    scores = jnp.dot(c_rows, b_rows.T, preferred_element_type=jnp.float32)
    length = running.shape[0]
    causal = (jnp.arange(length)[:, None] >= jnp.arange(length)[None, :])[:, :, None]
    decay_gap = jnp.where(causal, running[:, None, :] - running[None, :, :], 0.0)
    mixing = jnp.where(
        causal, jnp.exp(decay_gap) * scores[:, :, None] * steps_dt[None, :, :], 0.0
    ).astype(jnp.bfloat16)
    inside = jnp.einsum("tsh,shp->thp", mixing, values, preferred_element_type=jnp.float32)
    carried = jnp.exp(running[-1][None, :] - running) * steps_dt
    states = jnp.einsum(
        "sn,shp->hnp",
        b_rows.astype(jnp.float32),
        carried[:, :, None] * values.astype(jnp.float32),
        precision=lax.Precision.HIGHEST,
    )
    return (running, inside, states, jnp.exp(running[-1]))


def shards(
    residual,
    expert_rows,
    expert_ids,
    expert_slots,
    combine_weights,
    norm_gain,
    in_weight,
    conv_weight,
    conv_bias,
    bc_weight,
    dt_weight,
    dt_bias,
    decay_log,
    skip_gain,
):
    own_rows, width = residual.shape
    returned = lax.all_to_all(expert_rows, "exp", split_axis=2, concat_axis=1, tiled=True)
    capacity = returned.shape[3]
    buffers = returned.reshape(returned.shape[1] * capacity, width)
    picked = jnp.take(buffers, expert_ids * capacity + expert_slots, axis=0)
    mixture = jnp.zeros((own_rows, width), jnp.float32)
    for column in range(TOPK):
        mixture = mixture + combine_weights[:, column][:, None] * picked[:, column].astype(
            jnp.float32
        )
    stream = residual.astype(jnp.float32) + mixture
    factor = lax.rsqrt(jnp.mean(stream * stream, axis=1, keepdims=True) + 1e-06)
    normed = (stream * factor * norm_gain[None, :]).astype(jnp.bfloat16)
    group_rows = own_rows * lax.axis_size("exp")
    local_width = in_weight.shape[1]
    x_in = jnp.dot(
        lax.all_gather(normed, "exp", axis=0, tiled=True),
        in_weight,
        preferred_element_type=jnp.float32,
    ).astype(jnp.bfloat16)
    rim_rows = passed_along(x_in[group_rows - (KCONV - 1) :], "seq", 1)
    padded = jnp.concatenate([rim_rows, x_in], axis=0)
    filtered = jnp.zeros((group_rows, local_width), jnp.float32) + conv_bias[None, :]
    for tap in range(KCONV):
        filtered = filtered + conv_weight[tap][None, :] * padded[tap : tap + group_rows].astype(
            jnp.float32
        )
    activated = jax.nn.silu(filtered).astype(jnp.bfloat16)
    state_part = jnp.dot(activated, bc_weight, preferred_element_type=jnp.float32)
    rate_part = jnp.dot(activated, dt_weight, preferred_element_type=jnp.float32)
    state_proj, dt_raw = lax.psum((state_part, rate_part), "exp")
    heads_here = local_width // HEAD
    first_head = lax.axis_index("exp") * heads_here
    steps_dt = jax.nn.softplus(
        lax.dynamic_slice_in_dim(dt_raw, first_head, heads_here, 1) + dt_bias[None, :]
    )
    decays = -jnp.exp(decay_log)[None, :] * steps_dt
    b_all = state_proj[:, :NSTATE].astype(jnp.bfloat16)
    c_all = state_proj[:, NSTATE:].astype(jnp.bfloat16)
    blocks = group_rows // STRETCH
    c_blocks = c_all.reshape(blocks, STRETCH, NSTATE)
    value_blocks = activated.reshape(blocks, STRETCH, heads_here, HEAD)

    def advance(carry, inputs):
        local_states, prefix_decay = carry
        b_rows, c_rows, block_dt, block_decays, values = inputs
        running, inside, states, total = block_terms(b_rows, c_rows, block_dt, block_decays, values)
        return (
            (total[:, None, None] * local_states + states, prefix_decay * total),
            (running, inside, local_states, prefix_decay),
        )

    start_carry = (
        jnp.zeros((heads_here, NSTATE, HEAD), jnp.float32),
        jnp.ones((heads_here,), jnp.float32),
    )
    (final_states, device_decay), (runnings, insides, starts, prefixes) = lax.scan(
        advance,
        start_carry,
        (
            b_all.reshape(blocks, STRETCH, NSTATE),
            c_blocks,
            steps_dt.reshape(blocks, STRETCH, heads_here),
            decays.reshape(blocks, STRETCH, heads_here),
            value_blocks,
        ),
    )
    empty_states = jnp.zeros((heads_here, NSTATE, HEAD), jnp.float32)

    def relay_turn(turn, carried):
        incoming, outgoing = carried
        incoming = passed_along(outgoing, "seq", 1)
        return (incoming, device_decay[:, None, None] * incoming + final_states)

    incoming, outgoing_last = lax.fori_loop(
        0, lax.axis_size("seq") - 1, relay_turn, (empty_states, final_states)
    )
    entering = starts + prefixes[:, :, None, None] * incoming[None]
    across = jnp.exp(runnings)[:, :, :, None] * jnp.einsum(
        "btn,bhnp->bthp", c_blocks.astype(jnp.float32), entering, precision=lax.Precision.HIGHEST
    )
    output = insides + across + skip_gain[None, None, :, None] * value_blocks.astype(jnp.float32)
    return output.astype(jnp.bfloat16).reshape(group_rows, local_width)


def solution(mesh):
    placed = (
        P(("seq", "exp"), None),
        P("seq", "exp", None, None, None),
        P(("seq", "exp"), None),
        P(("seq", "exp"), None),
        P(("seq", "exp"), None),
        P(),
        P(None, "exp"),
        P(None, "exp"),
        P("exp"),
        P("exp", None),
        P("exp", None),
        P("exp"),
        P("exp"),
        P("exp"),
    )
    return jax.shard_map(
        shards, mesh=mesh, in_specs=placed, out_specs=P("seq", "exp"), check_vma=False
    )
```

profile of v0, /device:TPU:0, one launch (start us, length us, event | category | flops | bytes accessed | tf_op | source)
XLA Modules:
  0.0 608.4 jit_solution(3130771036729045118)
XLA Ops:
  6.5 7.3 %all-to-all-start = ((bf16[1,1,16,24,8192]{4,3,1,0,2:T(8,128)(2,1)}), bf16[1,1,16,24,8192]{4,3,1,0,2:T(8,128)(2,1)}, u32[]{:S(2)}, u32[]{:S(2)}) async-start(bf16[1,1,16,24,8192]{4,3,1,0,2:T(8,128)(2,1)} %bitcast.113), calls=%async_computation | async-start | bytes 12582912 | tf_op jit(solution)/shard_map/all_to_all | solution.py:56
  14.2 101.9 %all-to-all-done = bf16[1,1,16,24,8192]{4,3,1,0,2:T(8,128)(2,1)} async-done(((bf16[1,1,16,24,8192]{4,3,1,0,2:T(8,128)(2,1)}), bf16[1,1,16,24,8192]{4,3,1,0,2:T(8,128)(2,1)}, u32[]{:S(2)}, u32[]{:S(2)}) %all-to-all-start) | async-done | bytes 6291488 | tf_op jit(solution)/shard_map/all_to_all | solution.py:56
  116.2 12.6 %gather_fusion = bf16[256,8192]{1,0:T(8,128)(2,1)} fusion(bf16[384,8192]{1,0:T(8,128)(2,1)} %bitcast.3, s32[1024]{0:T(1024)S(1)} %pad_clamp_fusion), kind=kCustom, calls=%fused_computation | custom fusion | bytes 8389632 | tf_op jit(solution)/shard_map/jit(_take)/gather | solution.py:59
  128.8 7.6 %reshape.94 = bf16[128,2,8192]{2,1,0:T(2,128)(2,1)} reshape(bf16[256,8192]{1,0:T(8,128)(2,1)} %gather_fusion) | data formatting | bytes 8388608 | tf_op jit(solution)/shard_map/jit(_take)/gather | solution.py:59
  136.4 7.2 %copy_select_fusion = bf16[128,2,8192]{2,0,1:T(8,128)(2,1)S(1)} fusion(bf16[128,2,8192]{2,1,0:T(2,128)(2,1)} %reshape.94, pred[128,2]{0,1:T(4,128)(4,1)S(1)} %get-tuple-element.250), kind=kLoop, calls=%fused_computation.47 | loop fusion | flops 2097152 | bytes 8388864 | tf_op jit(solution)/shard_map/jit(_take)/select_n | solution.py:59
  143.6 1.4 multiply_reduce_fusion
  145.0 3.0 multiply_convert_fusion.1
  148.1 203.5 %all-gather.2.cloned.1.call-done = bf16[2048,8192]{1,0:T(8,128)(2,1)} async-done(((bf16[128,8192]{1,0:T(8,128)(2,1)}), bf16[2048,8192]{1,0:T(8,128)(2,1)}) %all-gather.2.cloned.1.call-update) | async-done | bytes 33554448 | tf_op jit(solution)/shard_map/all_gather | solution.py:71
  351.7 23.8 %convolution_convert_fusion = bf16[2048,512]{1,0:T(8,128)(2,1)S(1)} fusion(bf16[2048,8192]{1,0:T(8,128)(2,1)} %all-gather.2.cloned.1.call-done, bf16[8192,512]{1,0:T(8,128)(2,1)} %param.24), kind=kOutput, calls=%fused_computation.52 | convolution fusion | flops 17180917760 | bytes 44040192 | tf_op jit(solution)/shard_map/dot_general | solution.py:70
  375.4 1.3 copy-done.4
  376.8 1.7 collective-permute-start.1
  379.3 6.0 multiply_convert_fusion
  385.3 1.8 fusion.34
  387.1 1.7 fusion.35
  388.8 3.6 reshape.109
  392.5 4.0 copy.57
  396.5 88.4 %all-reduce.4 = bf16[2048,128]{1,0:T(8,128)(2,1)S(1)} all-reduce(f32[2048,128]{1,0:T(8,128)} %fusion.35), channel_id=1, replica_groups=mesh['seq'=8,'exp'=16] {'exp'}, use_global_device_ids=true, to_apply=%region_1.2 | all-reduce | flops 262144 | bytes 1572864 | tf_op jit(solution)/shard_map/psum | solution.py:85
  486.0 1.2 copy.58
  488.2 38.5 %while.34 = (s32[]{:T(128)}, f32[8,64,64]{1,2,0:T(8,128)S(1)}, f32[8]{0:T(128)S(1)}, f32[8,256,8]{1,2,0:T(8,128)}, f32[8,256,8,64]{1,3,2,0:T(8,128)}, /*index=5*...) while((s32[]{:T(128)}, f32[8,64,64]{1,2,0:T(8,128)S(1)}, ...), condition=%wide.region_6.7_spmd.clone, body=%wide.region_3.6_spmd.clone.sunk | while | flops 180033568 | bytes 2758157 | solution.py:111
  489.5 1.6 fusion.62
  494.3 1.6 fusion.62
  499.2 1.6 fusion.62
  504.0 1.6 fusion.62
  508.8 1.6 fusion.62
  513.6 1.6 fusion.62
  518.4 1.6 fusion.62
  523.2 1.5 fusion.62
  526.9 55.2 %while.33 = (s32[]{:T(128)}, f32[8,64,64]{2,1,0:T(8,128)}, f32[8,64,64]{2,1,0:T(8,128)S(1)}, f32[8]{0:T(128)S(1)}, f32[8,64,64]{2,1,0:T(8,128)S(1)}, /*index=5*/s32[]{:T(128)}) while((s32[]{:T(128)}, f32[8,64,64]{2,1,0:T(8,128)}, f32[8,64,64]{2,1,0:T(8,128)S(1)}, f32[8]{0:T(128)S(1)}, f32[8,64,64]{2,1,0:T(8,128)S(1)}, ...), condition=%wide.region_8.9_spmd, body=%wide.region_7.8_spmd.sunk | while | flops 65538 | bytes 1441961 | solution.py:129
  526.9 1.3 collective-permute-start
  528.2 1.1 collective-permute-done
  530.0 8.3 %collective-permute-start = (f32[8,64,64]{2,1,0:T(8,128)S(1)}, f32[8,64,64]{2,1,0:T(8,128)S(1)}, u32[]{:S(2)}, u32[]{:S(2)}) collective-permute-start(f32[8,64,64]{2,1,0:T(8,128)S(1)} %get-tuple-element.428), channel_id=1, source_target_pairs={{0,16},{16,32},{32,48},{48,64},{64,80},{80,96},{96,112},{1,17},{17... | collective-permute-start | bytes 393224 | tf_op jit(solution)/shard_map/while/body/eval_jaxpr/ppermute | solution.py:16
  538.3 1.1 collective-permute-done
  540.2 6.5 %collective-permute-start = (f32[8,64,64]{2,1,0:T(8,128)S(1)}, f32[8,64,64]{2,1,0:T(8,128)S(1)}, u32[]{:S(2)}, u32[]{:S(2)}) collective-permute-start(f32[8,64,64]{2,1,0:T(8,128)S(1)} %get-tuple-element.428), channel_id=1, source_target_pairs={{0,16},{16,32},{32,48},{48,64},{64,80},{80,96},{96,112},{1,17},{17... | collective-permute-start | bytes 393224 | tf_op jit(solution)/shard_map/while/body/eval_jaxpr/ppermute | solution.py:16
  546.7 1.1 collective-permute-done
  548.5 6.5 %collective-permute-start = (f32[8,64,64]{2,1,0:T(8,128)S(1)}, f32[8,64,64]{2,1,0:T(8,128)S(1)}, u32[]{:S(2)}, u32[]{:S(2)}) collective-permute-start(f32[8,64,64]{2,1,0:T(8,128)S(1)} %get-tuple-element.428), channel_id=1, source_target_pairs={{0,16},{16,32},{32,48},{48,64},{64,80},{80,96},{96,112},{1,17},{17... | collective-permute-start | bytes 393224 | tf_op jit(solution)/shard_map/while/body/eval_jaxpr/ppermute | solution.py:16
  555.1 1.1 collective-permute-done
  556.9 6.5 %collective-permute-start = (f32[8,64,64]{2,1,0:T(8,128)S(1)}, f32[8,64,64]{2,1,0:T(8,128)S(1)}, u32[]{:S(2)}, u32[]{:S(2)}) collective-permute-start(f32[8,64,64]{2,1,0:T(8,128)S(1)} %get-tuple-element.428), channel_id=1, source_target_pairs={{0,16},{16,32},{32,48},{48,64},{64,80},{80,96},{96,112},{1,17},{17... | collective-permute-start | bytes 393224 | tf_op jit(solution)/shard_map/while/body/eval_jaxpr/ppermute | solution.py:16
  563.5 1.1 collective-permute-done
  565.3 6.5 %collective-permute-start = (f32[8,64,64]{2,1,0:T(8,128)S(1)}, f32[8,64,64]{2,1,0:T(8,128)S(1)}, u32[]{:S(2)}, u32[]{:S(2)}) collective-permute-start(f32[8,64,64]{2,1,0:T(8,128)S(1)} %get-tuple-element.428), channel_id=1, source_target_pairs={{0,16},{16,32},{32,48},{48,64},{64,80},{80,96},{96,112},{1,17},{17... | collective-permute-start | bytes 393224 | tf_op jit(solution)/shard_map/while/body/eval_jaxpr/ppermute | solution.py:16
  571.8 1.1 collective-permute-done
  573.7 6.5 %collective-permute-start = (f32[8,64,64]{2,1,0:T(8,128)S(1)}, f32[8,64,64]{2,1,0:T(8,128)S(1)}, u32[]{:S(2)}, u32[]{:S(2)}) collective-permute-start(f32[8,64,64]{2,1,0:T(8,128)S(1)} %get-tuple-element.428), channel_id=1, source_target_pairs={{0,16},{16,32},{32,48},{48,64},{64,80},{80,96},{96,112},{1,17},{17... | collective-permute-start | bytes 393224 | tf_op jit(solution)/shard_map/while/body/eval_jaxpr/ppermute | solution.py:16
  580.2 1.1 collective-permute-done
  582.0 1.1 copy.61
  583.1 1.8 multiply_add_fusion.1
  585.0 1.8 fusion.36
  587.2 2.8 add_convert_fusion
  590.0 5.1 copy.67
  595.1 6.4 %reshape.108 = bf16[2048,512]{1,0:T(8,128)(2,1)} reshape(bf16[8,256,8,64]{3,2,1,0:T(8,128)(2,1)} %copy.67) | data formatting | bytes 4194304 | tf_op jit(solution)/shard_map/reshape | solution.py:137
  (197 shorter events, 34.3 us)
Async XLA Ops:
  6.5 378.8 %copy-start = (bf16[512,128]{1,0:T(8,128)(2,1)S(1)}, bf16[512,128]{1,0:T(8,128)(2,1)}, u32[]{:S(2)}) copy-start(bf16[512,128]{1,0:T(8,128)(2,1)} %param.28) | copy-start | bytes 393220
  6.5 7.4 %copy-start.10 = (s32[128,2]{0,1:T(2,128)S(1)}, s32[128,2]{0,1:T(2,128)}, u32[]{:S(2)}) copy-start(s32[128,2]{0,1:T(2,128)} %param.21) | copy-start | bytes 3076
  6.5 7.4 %copy-start.11 = (s32[128,2]{0,1:T(2,128)S(1)}, s32[128,2]{0,1:T(2,128)}, u32[]{:S(2)}) copy-start(s32[128,2]{0,1:T(2,128)} %param.20) | copy-start | bytes 3076
  6.5 7.7 %copy-start.12 = (f32[128,2]{0,1:T(2,128)S(1)}, f32[128,2]{0,1:T(2,128)}, u32[]{:S(2)}) copy-start(f32[128,2]{0,1:T(2,128)} %param.22) | copy-start | bytes 3076
  6.5 109.6 %all-to-all-start = ((bf16[1,1,16,24,8192]{4,3,1,0,2:T(8,128)(2,1)}), bf16[1,1,16,24,8192]{4,3,1,0,2:T(8,128)(2,1)}, u32[]{:S(2)}, u32[]{:S(2)}) async-start(bf16[1,1,16,24,8192]{4,3,1,0,2:T(8,128)(2,1)} %bitcast.113), calls=%async_computation | async-start | bytes 12582912 | tf_op jit(solution)/shard_map/all_to_all | solution.py:56
  13.9 337.8 %all-gather.2.cloned.1.call-start = ((), (), s32[]{:S(2)}) async-start(), calls=%async_computation.1 | async-start | bytes 35651584 | tf_op jit(solution)/shard_map/all_gather | solution.py:71
  136.4 7.2 %copy-start.2 = (bf16[128,8192]{1,0:T(8,128)(2,1)S(1)}, bf16[128,8192]{1,0:T(8,128)(2,1)}, u32[]{:S(2)}) copy-start(bf16[128,8192]{1,0:T(8,128)(2,1)} %param.18) | copy-start | bytes 6291460
  143.6 1.4 copy-start.7
  145.0 3.1 copy-start.8
  148.0 339.2 %all-reduce.3.cloned.1.call-start = ((), (), s32[]{:S(2)}) async-start(), calls=%async_computation.2 | async-start | bytes 2097152 | tf_op jit(solution)/shard_map/psum | solution.py:85
  148.1 230.4 %copy-start.15 = (f32[8]{0:T(128)S(1)}, f32[8]{0:T(128)}, u32[]{:S(2)}) copy-start(f32[8]{0:T(128)} %param.30) | copy-start | bytes 100
  148.1 231.2 %copy-start.9 = (f32[512]{0:T(512)S(1)}, f32[512]{0:T(512)}, u32[]{:S(2)}) copy-start(f32[512]{0:T(512)} %param.26) | copy-start | bytes 6148
  375.4 1.3 copy-start.4
  376.8 2.5 collective-permute-start.1
  379.3 7.8 %copy-start.5 = (bf16[512,128]{1,0:T(8,128)(2,1)S(1)}, bf16[512,128]{1,0:T(8,128)(2,1)}, u32[]{:S(2)}) copy-start(bf16[512,128]{1,0:T(8,128)(2,1)} %param.27) | copy-start | bytes 393220
  392.5 94.7 %copy-start.13 = (f32[8]{0:T(128)S(1)}, f32[8]{0:T(128)}, u32[]{:S(2)}) copy-start(f32[8]{0:T(128)} %param.29) | copy-start | bytes 100
  526.9 2.4 collective-permute-start
  529.3 0.7 copy-start.1
  530.0 9.4 %collective-permute-start = (f32[8,64,64]{2,1,0:T(8,128)S(1)}, f32[8,64,64]{2,1,0:T(8,128)S(1)}, u32[]{:S(2)}, u32[]{:S(2)}) collective-permute-start(f32[8,64,64]{2,1,0:T(8,128)S(1)} %get-tuple-element.428), channel_id=1, source_target_pairs={{0,16},{16,32},{32,48},{48,64},{64,80},{80,96},{96,112},{1,17},{17... | collective-permute-start | bytes 393224 | tf_op jit(solution)/shard_map/while/body/eval_jaxpr/ppermute | solution.py:16
  539.5 0.7 copy-start.1
  540.2 7.7 %collective-permute-start = (f32[8,64,64]{2,1,0:T(8,128)S(1)}, f32[8,64,64]{2,1,0:T(8,128)S(1)}, u32[]{:S(2)}, u32[]{:S(2)}) collective-permute-start(f32[8,64,64]{2,1,0:T(8,128)S(1)} %get-tuple-element.428), channel_id=1, source_target_pairs={{0,16},{16,32},{32,48},{48,64},{64,80},{80,96},{96,112},{1,17},{17... | collective-permute-start | bytes 393224 | tf_op jit(solution)/shard_map/while/body/eval_jaxpr/ppermute | solution.py:16
  547.8 0.7 copy-start.1
  548.5 7.7 %collective-permute-start = (f32[8,64,64]{2,1,0:T(8,128)S(1)}, f32[8,64,64]{2,1,0:T(8,128)S(1)}, u32[]{:S(2)}, u32[]{:S(2)}) collective-permute-start(f32[8,64,64]{2,1,0:T(8,128)S(1)} %get-tuple-element.428), channel_id=1, source_target_pairs={{0,16},{16,32},{32,48},{48,64},{64,80},{80,96},{96,112},{1,17},{17... | collective-permute-start | bytes 393224 | tf_op jit(solution)/shard_map/while/body/eval_jaxpr/ppermute | solution.py:16
  556.2 0.7 copy-start.1
  556.9 7.7 %collective-permute-start = (f32[8,64,64]{2,1,0:T(8,128)S(1)}, f32[8,64,64]{2,1,0:T(8,128)S(1)}, u32[]{:S(2)}, u32[]{:S(2)}) collective-permute-start(f32[8,64,64]{2,1,0:T(8,128)S(1)} %get-tuple-element.428), channel_id=1, source_target_pairs={{0,16},{16,32},{32,48},{48,64},{64,80},{80,96},{96,112},{1,17},{17... | collective-permute-start | bytes 393224 | tf_op jit(solution)/shard_map/while/body/eval_jaxpr/ppermute | solution.py:16
  564.6 0.7 copy-start.1
  565.3 7.7 %collective-permute-start = (f32[8,64,64]{2,1,0:T(8,128)S(1)}, f32[8,64,64]{2,1,0:T(8,128)S(1)}, u32[]{:S(2)}, u32[]{:S(2)}) collective-permute-start(f32[8,64,64]{2,1,0:T(8,128)S(1)} %get-tuple-element.428), channel_id=1, source_target_pairs={{0,16},{16,32},{32,48},{48,64},{64,80},{80,96},{96,112},{1,17},{17... | collective-permute-start | bytes 393224 | tf_op jit(solution)/shard_map/while/body/eval_jaxpr/ppermute | solution.py:16
  573.0 0.7 copy-start.1
  573.7 7.7 %collective-permute-start = (f32[8,64,64]{2,1,0:T(8,128)S(1)}, f32[8,64,64]{2,1,0:T(8,128)S(1)}, u32[]{:S(2)}, u32[]{:S(2)}) collective-permute-start(f32[8,64,64]{2,1,0:T(8,128)S(1)} %get-tuple-element.428), channel_id=1, source_target_pairs={{0,16},{16,32},{32,48},{48,64},{64,80},{80,96},{96,112},{1,17},{17... | collective-permute-start | bytes 393224 | tf_op jit(solution)/shard_map/while/body/eval_jaxpr/ppermute | solution.py:16
  581.4 0.7 copy-start.1
  585.0 1.9 copy-start.6
  585.0 2.2 copy-start.3
  585.0 2.2 copy-start.14
Sparse Core Ops, SparseCore 0:
  148.2 203.4 all-gather.1
  387.2 90.1 all-reduce.2
where the time goes:
time: 615 us; the launch traced here: 608 us
  waiting for transfers between devices  314 us (51%)
  blocking collectives  88.4 us (14%)
  local copies, waits for them, and re-layouts  52.2 us (8%)
  starting transfers between devices  51.4 us (8%)
  matrix products  46.7 us (8%)
  other arithmetic  41.4 us (7%)
  between operations  13.8 us (2%)
    all_gather x1, waiting for transfers between devices, shards(): lax.all_gather(normed, 'exp', axis=0, tiled=True)  204 us
    all_to_all x1, waiting for transfers between devices, shards(): lax.all_to_all(expert_rows, 'exp', split_axis=2, concat_axis=1, tiled=True)  102 us
    psum x1, blocking collectives, shards(): state_proj, dt_raw = lax.psum((state_part, rate_part), 'exp')  88.4 us
    ppermute x8, starting transfers between devices, passed_along(): lax.ppermute(value, axis, [(source, source + steps) for source in range(l...  44 us
    dot_general x1, matrix products, shards(): jnp.dot(lax.all_gather(normed, 'exp', axis=0, tiled=True), in_weight, pre...  23.8 us
    gather x2, local copies, waits for them, and re-layouts, shards(): picked = jnp.take(buffers, expert_ids * capacity + expert_slots, axis=0)  20.2 us
    dot_general x8, matrix products, block_terms(): jnp.einsum('tsh,shp->thp', mixing, values, preferred_element_type=jnp.flo...  12.5 us
  transfers between devices with their start and end apart: 11, of which 10 were waited for; matrix products, arithmetic and copies ran while one was open for 2% of the time, Pallas kernels for 0%

commit v1 on v0

v1 whole, which is shorter than its diff:
```python
import jax
import jax.numpy as jnp
from jax import lax
from jax.experimental import pallas as pl
from jax.experimental.pallas import tpu as pltpu
from jax.sharding import Mesh, PartitionSpec as P

TOPK = 2
KCONV = 4
HEAD = 64
NSTATE = 64
STRETCH = 256
EPS = 1e-06
SPAN = ("z", "c")
PLANE = ("x", "y")
BF16 = jnp.bfloat16
F32 = jnp.float32
EXACT = lax.Precision.HIGHEST


def shifted(value, axis, steps):
    count = lax.axis_size(axis)
    return lax.ppermute(value, axis, [(i, (i + steps) % count) for i in range(count)])


def passed_on(value, axes, steps):
    count = lax.axis_size(axes)
    return lax.ppermute(value, axes, [(i, i + steps) for i in range(count - steps)])


def whole(shape):
    return pl.BlockSpec(shape, lambda *_: (0,) * len(shape))


def dot(a, b, dims=((1,), (0,)), precision=None):
    return lax.dot_general(a, b, (dims, ((), ())), precision=precision, preferred_element_type=F32)


def combine_body(index_ref, weight_ref, rows_ref, residual_ref, gain_ref, out_ref, stream_ref):
    own, width = residual_ref.shape
    slots = rows_ref.shape[0]
    step = 1024
    lane = lax.broadcasted_iota(jnp.int32, (own, slots), 1)
    mix = jnp.zeros((own, slots), F32)
    for k in range(TOPK):
        mix = mix + jnp.where(lane == index_ref[:, k : k + 1], weight_ref[:, k : k + 1], 0.0)
    high = mix.astype(BF16)
    low = (mix - high.astype(F32)).astype(BF16)

    def gather(i, total):
        cols = pl.ds(pl.multiple_of(i * step, step), step)
        rows = rows_ref[:, cols]
        stream = residual_ref[:, cols].astype(F32) + (dot(high, rows) + dot(low, rows))
        stream_ref[:, cols] = stream
        return total + jnp.sum(stream * stream, axis=1, keepdims=True)

    total = lax.fori_loop(0, width // step, gather, jnp.zeros((own, 1), F32))
    factor = lax.rsqrt(total / width + EPS)

    def scale(i, carry):
        cols = pl.ds(pl.multiple_of(i * step, step), step)
        out_ref[:, cols] = (stream_ref[:, cols] * factor * gain_ref[:, cols]).astype(BF16)
        return carry

    lax.fori_loop(0, width // step, scale, 0)


def combine(index, weights, rows, residual, gain):
    own, width = residual.shape
    return pl.pallas_call(
        combine_body,
        name="combine",
        out_shape=jax.ShapeDtypeStruct((own, width), BF16),
        scratch_shapes=[pltpu.VMEM((own, width), F32)],
    )(index, weights, rows, residual, gain.reshape(1, width))


def project_body(*refs):
    *x_refs, w_ref, out_ref, acc_ref = refs
    k = pl.program_id(1)
    depth = w_ref.shape[-2]
    rows = x_refs[0].shape[0]
    cols = pl.ds(pl.multiple_of(k * depth, depth), depth)
    left = jnp.concatenate([ref[:, cols] for ref in x_refs], axis=0)
    part = dot(left, w_ref[...].reshape(w_ref.shape[-2:]))

    @pl.when(k == 0)
    def _():
        acc_ref[...] = part

    @pl.when(k > 0)
    def _():
        acc_ref[...] += part

    @pl.when(k == pl.num_programs(1) - 1)
    def _():
        for u in range(len(x_refs)):
            out_ref[0, u] = acc_ref[u * rows : (u + 1) * rows].astype(BF16)


def project(units, weight, weight_spec, shards, depth_steps):
    rows, width = units[0].shape
    cols = weight.shape[-1]
    return pl.pallas_call(
        project_body,
        name="project",
        grid=(shards, depth_steps),
        in_specs=[whole((rows, width)) for _ in units] + [weight_spec],
        out_specs=pl.BlockSpec((1, len(units), rows, cols), lambda r, k: (r, 0, 0, 0)),
        out_shape=jax.ShapeDtypeStruct((shards, len(units), rows, cols), BF16),
        scratch_shapes=[pltpu.VMEM((len(units) * rows, cols), F32)],
    )(*units, weight)


def filter_body(place_ref, near_ref, far_ref, rim_ref, taps_ref, weight_ref, act_ref, part_ref, pad_ref):
    r = pl.program_id(0)
    near, rows, cols = near_ref.shape[1:]
    y = place_ref[0]
    order = (0, 1, 3)
    units = near + 1
    pad_ref[0:8] = rim_ref[0].astype(F32)
    for u in range(near):
        at = (y + order[u]) % units
        pad_ref[pl.ds(pl.multiple_of(8 + at * rows, 8), rows)] = near_ref[0, u].astype(F32)
    at = (y + 2) % units
    pad_ref[pl.ds(pl.multiple_of(8 + at * rows, 8), rows)] = far_ref[0, 0].astype(F32)
    total = units * rows
    step = 128
    for i in range(total // step):
        filtered = taps_ref[0, KCONV : KCONV + 1, :]
        for tap in range(KCONV):
            first = 8 - (KCONV - 1) + tap + i * step
            filtered = filtered + taps_ref[0, tap : tap + 1, :] * pad_ref[first : first + step]
        act_ref[0, i * step : (i + 1) * step] = jax.nn.silu(filtered).astype(BF16)
    part = dot(act_ref[0], weight_ref[0])

    @pl.when(r == 0)
    def _():
        part_ref[...] = part

    @pl.when(r > 0)
    def _():
        part_ref[...] += part


def filter_rows(y, near, far, rim, taps, weights):
    shards, n_near, rows, cols = near.shape
    total = (n_near + 1) * rows
    maps = weights.shape[-1]
    return pl.pallas_call(
        filter_body,
        name="filter",
        grid_spec=pltpu.PrefetchScalarGridSpec(
            num_scalar_prefetch=1,
            grid=(shards,),
            in_specs=[
                pl.BlockSpec((1, n_near, rows, cols), lambda r, _: (r, 0, 0, 0)),
                pl.BlockSpec((1, 1, rows, cols), lambda r, _: (r, 0, 0, 0)),
                pl.BlockSpec((1, 8, cols), lambda r, _: (r, 0, 0)),
                pl.BlockSpec((1, 8, cols), lambda r, _: (r, 0, 0)),
                pl.BlockSpec((1, cols, maps), lambda r, _: (r, 0, 0)),
            ],
            out_specs=[
                pl.BlockSpec((1, total, cols), lambda r, _: (r, 0, 0)),
                pl.BlockSpec((total, maps), lambda r, _: (0, 0)),
            ],
            scratch_shapes=[pltpu.VMEM((total + 8, cols), F32)],
        ),
        out_shape=[
            jax.ShapeDtypeStruct((shards, total, cols), BF16),
            jax.ShapeDtypeStruct((total, maps), F32),
        ],
    )(y.reshape(1), near, far, rim, taps, weights)


def wide(narrow, spread):
    return dot(narrow, spread, precision=EXACT)


def rates_of(rate_rows, choice, head_row):
    raw = wide(rate_rows, choice)
    step = jax.nn.softplus(raw + head_row[0:1])
    return step, -jnp.exp(head_row[1:2]) * step


def lower(n):
    return (
        lax.broadcasted_iota(jnp.int32, (n, n), 0) >= lax.broadcasted_iota(jnp.int32, (n, n), 1)
    ).astype(F32)


def state_body(place_ref, maps_ref, act_ref, choice_ref, spread_ref, head_ref, start_ref, run_ref, final_ref, state_ref, sum_ref):
    b = pl.program_id(0)
    n = act_ref.shape[1]

    @pl.when(b == 0)
    def _():
        state_ref[...] = jnp.zeros_like(state_ref)
        sum_ref[...] = jnp.zeros_like(sum_ref)

    maps = maps_ref[...].reshape(n, maps_ref.shape[-1])
    step, decay = rates_of(maps[:, 2 * NSTATE :], choice_ref[...], head_ref[...])
    running = dot(lower(n), decay, precision=EXACT)
    total = running[n - 1 : n]
    spread = spread_ref[...]
    carried = wide(jnp.exp(total - running) * step, spread) * act_ref[0].astype(F32)
    high = carried.astype(BF16)
    low = (carried - high.astype(F32)).astype(BF16)
    b_rows = maps[:, :NSTATE].astype(BF16)
    state = dot(b_rows, high, ((0,), (0,))) + dot(b_rows, low, ((0,), (0,)))
    run_ref[...] = sum_ref[0:1] + running
    start_ref[0] = state_ref[...]
    state_ref[...] = wide(jnp.broadcast_to(jnp.exp(total), (8, total.shape[1])), spread)[0:1] * state_ref[...] + state
    sum_ref[...] = sum_ref[...] + total

    @pl.when(b == pl.num_programs(0) - 1)
    def _():
        final_ref[0:NSTATE] = state_ref[...]
        final_ref[NSTATE : NSTATE + 8] = wide(jnp.exp(sum_ref[...]), spread)


def inside_body(place_ref, maps_ref, act_ref, choice_ref, choice_t_ref, spread_ref, head_ref, head_t_ref, skip_ref, start_ref, out_ref):
    n = act_ref.shape[1]
    half = n // 2
    maps = maps_ref[...].reshape(n, maps_ref.shape[-1])
    rates = maps[:, 2 * NSTATE :]
    step, decay = rates_of(rates, choice_ref[...], head_ref[...])
    tri = lower(n)
    running = dot(tri, decay, precision=EXACT)
    raw_t = dot(choice_t_ref[...], rates, ((1,), (1,)), precision=EXACT)
    step_t = jax.nn.softplus(raw_t + head_t_ref[:, 0:1])
    decay_t = -jnp.exp(head_t_ref[:, 1:2]) * step_t
    running_t = dot(decay_t, tri, ((1,), (1,)), precision=EXACT)
    b_rows = maps[:, :NSTATE].astype(BF16)
    c_rows = maps[:, NSTATE : 2 * NSTATE].astype(BF16)
    scores = tri * dot(c_rows, b_rows, ((1,), (1,)))
    start = start_ref[0]
    high = start.astype(BF16)
    low = (start - high.astype(F32)).astype(BF16)
    across = dot(c_rows, high) + dot(c_rows, low)
    act = act_ref[0]
    base = wide(jnp.exp(running), spread_ref[...]) * across + skip_ref[...] * act.astype(F32)
    heads = act.shape[1] // HEAD
    first = lax.broadcasted_iota(jnp.int32, (1, 2 * HEAD), 1) < HEAD
    for pair in range(heads // 2):
        cols = slice(2 * HEAD * pair, 2 * HEAD * (pair + 1))
        values = act[:, cols]
        tops, bottoms = [], []
        for h in (2 * pair, 2 * pair + 1):
            row, gain = running_t[h : h + 1], step_t[h : h + 1]
            column = running[:, h : h + 1]
            top = jnp.exp(jnp.minimum(column[:half] - row[:, :half], 0.0)) * scores[:half, :half] * gain[:, :half]
            bottom = jnp.exp(jnp.minimum(column[half:] - row, 0.0)) * scores[half:] * gain
            tops.append(dot(top.astype(BF16), values[:half]))
            bottoms.append(dot(bottom.astype(BF16), values))
        out_ref[:half, cols] = base[:half, cols] + jnp.where(first, tops[0], tops[1])
        out_ref[half:, cols] = base[half:, cols] + jnp.where(first, bottoms[0], bottoms[1])


def finish_body(inside_ref, maps_ref, run_ref, spread_ref, entering_ref, out_ref):
    n = inside_ref.shape[0]
    maps = maps_ref[...].reshape(n, maps_ref.shape[-1])
    c_rows = maps[:, NSTATE : 2 * NSTATE].astype(BF16)
    entering = entering_ref[...]
    high = entering.astype(BF16)
    low = (entering - high.astype(F32)).astype(BF16)
    across = dot(c_rows, high) + dot(c_rows, low)
    out_ref[...] = (inside_ref[...] + wide(jnp.exp(run_ref[...]), spread_ref[...]) * across).astype(BF16)


def scan_output(x, maps, act, dt_bias, decay_log, skip_gain, e):
    subs, rows, cols = act.shape
    tokens = subs * rows
    blocks = tokens // STRETCH
    inner = rows // STRETCH
    heads = cols // HEAD
    n_maps = maps.shape[1]
    lanes = n_maps - 2 * NSTATE
    head = lax.broadcasted_iota(jnp.int32, (lanes, lanes), 0)
    lane = lax.broadcasted_iota(jnp.int32, (lanes, lanes), 1)
    choice = ((head == lane + e * heads) & (lane < heads)).astype(F32)
    choice_t = (
        lax.broadcasted_iota(jnp.int32, (heads, lanes), 1)
        == lax.broadcasted_iota(jnp.int32, (heads, lanes), 0) + e * heads
    ).astype(F32)
    spread = (
        lax.broadcasted_iota(jnp.int32, (lanes, cols), 0)
        == lax.broadcasted_iota(jnp.int32, (lanes, cols), 1) // HEAD
    ).astype(F32)
    per_head = jnp.stack([dt_bias, decay_log])
    head_row = jnp.pad(per_head, ((0, 6), (0, lanes - heads)))
    head_t = jnp.pad(per_head.T, ((0, 0), (0, lanes - 2)))
    skip = jnp.repeat(skip_gain, HEAD)[None, :]
    place = x.reshape(1)

    maps_spec = pl.BlockSpec((STRETCH, n_maps), lambda b, *_: (b, 0))
    act_spec = pl.BlockSpec((1, STRETCH, cols), lambda b, p: ((p[0] + subs - b // inner) % subs, b % inner, 0))
    start_spec = pl.BlockSpec((1, NSTATE, cols), lambda b, *_: (b, 0, 0))
    lane_spec = pl.BlockSpec((STRETCH, lanes), lambda b, *_: (b, 0))
    wide_spec = pl.BlockSpec((STRETCH, cols), lambda b, *_: (b, 0))
    start, runs, final = pl.pallas_call(
        state_body,
        name="states",
        grid_spec=pltpu.PrefetchScalarGridSpec(
            num_scalar_prefetch=1,
            grid=(blocks,),
            in_specs=[maps_spec, act_spec, whole((lanes, lanes)), whole((lanes, cols)), whole((8, lanes))],
            out_specs=[start_spec, lane_spec, whole((NSTATE + 8, cols))],
            scratch_shapes=[pltpu.VMEM((NSTATE, cols), F32), pltpu.VMEM((8, lanes), F32)],
        ),
        out_shape=[
            jax.ShapeDtypeStruct((blocks, NSTATE, cols), F32),
            jax.ShapeDtypeStruct((tokens, lanes), F32),
            jax.ShapeDtypeStruct((NSTATE + 8, cols), F32),
        ],
    )(place, maps, act, choice, spread, head_row)

    gone = [passed_on(final, SPAN, d) for d in range(1, lax.axis_size(SPAN))]

    inside = pl.pallas_call(
        inside_body,
        name="inside",
        grid_spec=pltpu.PrefetchScalarGridSpec(
            num_scalar_prefetch=1,
            grid=(blocks,),
            in_specs=[
                maps_spec,
                act_spec,
                whole((lanes, lanes)),
                whole((heads, lanes)),
                whole((lanes, cols)),
                whole((8, lanes)),
                whole((heads, lanes)),
                whole((1, cols)),
                start_spec,
            ],
            out_specs=wide_spec,
        ),
        out_shape=jax.ShapeDtypeStruct((tokens, cols), F32),
    )(place, maps, act, choice, choice_t, spread, head_row, head_t, skip, start)

    entering = gone[0][:NSTATE]
    decay = gone[0][NSTATE : NSTATE + 1]
    for block in gone[1:]:
        entering = entering + decay * block[:NSTATE]
        decay = decay * block[NSTATE : NSTATE + 1]

    return pl.pallas_call(
        finish_body,
        name="finish",
        grid=(blocks,),
        in_specs=[wide_spec, maps_spec, lane_spec, whole((lanes, cols)), whole((NSTATE, cols))],
        out_specs=wide_spec,
        out_shape=jax.ShapeDtypeStruct((tokens, cols), BF16),
    )(inside, maps, runs, spread, entering)


def shards(
    residual,
    expert_rows,
    expert_ids,
    expert_slots,
    combine_weights,
    norm_gain,
    in_weight,
    conv_weight,
    conv_bias,
    bc_weight,
    dt_weight,
    dt_bias,
    decay_log,
    skip_gain,
):
    own, width = residual.shape
    spans = lax.axis_size(SPAN)
    nx, ny = lax.axis_size("x"), lax.axis_size("y")
    s, e, x, y = (lax.axis_index(axis) for axis in (SPAN, PLANE, "x", "y"))
    local = in_weight.shape[1]
    depth = width // spans

    piece = lax.dynamic_slice_in_dim(in_weight, s * depth, depth, 0)
    pieces = [shifted(piece, "x", -r) for r in range(1, nx)]
    maps_weight = jnp.concatenate([bc_weight, dt_weight], axis=1)
    taps = jnp.concatenate([conv_weight, conv_bias[None], jnp.zeros((7 - KCONV, local), F32)], axis=0)
    maps_weights = jnp.stack([maps_weight] + [shifted(maps_weight, "x", -r) for r in range(1, nx)])
    all_taps = jnp.stack([taps] + [shifted(taps, "x", -r) for r in range(1, nx)])
    others = lax.all_gather(jnp.stack(pieces), SPAN)

    returned = lax.all_to_all(expert_rows, PLANE, split_axis=2, concat_axis=1, tiled=True)
    capacity = returned.shape[3]
    rows = returned.reshape(returned.shape[1] * capacity, width)
    normed = combine(expert_ids * capacity + expert_slots, combine_weights, rows, residual, norm_gain)

    below = shifted(normed, "y", 1)
    above = shifted(normed, "y", -1)
    half = own // 2
    far = jnp.concatenate([shifted(below[:half], "y", 1), shifted(above[half:], "y", -1)], axis=0)

    own_spec = pl.BlockSpec((depth, local), lambda r, k: (k, 0))
    other_spec = pl.BlockSpec((1, 1, depth, local), lambda r, k: (k, r, 0, 0))
    near = (normed, above, below)
    near_in = jnp.concatenate(
        [project(near, in_weight, own_spec, 1, spans), project(near, others, other_spec, nx - 1, spans)], axis=0
    )
    far_in = jnp.concatenate(
        [project((far,), in_weight, own_spec, 1, spans), project((far,), others, other_spec, nx - 1, spans)], axis=0
    )

    ends = jnp.stack([near_in[:, 0, -8:], near_in[:, 1, -8:], far_in[:, 0, -8:], near_in[:, 2, -8:]], axis=0)
    last = lax.dynamic_index_in_dim(ends, (ny - 1 - y) % ny, 0, keepdims=False)
    rim = passed_on(jnp.roll(last, -1, axis=0), SPAN + ("x",), 1)
    act, part = filter_rows(y, near_in, far_in, rim, all_taps, maps_weights)

    act_here = jnp.stack([act[0]] + [shifted(act[r], "x", r) for r in range(1, nx)])

    part = part.reshape(ny, own, part.shape[1])
    mine = lax.dynamic_index_in_dim(part, y, 0, keepdims=False)
    for d in range(1, ny):
        mine = mine + shifted(lax.dynamic_index_in_dim(part, (y + d) % ny, 0, keepdims=False), "y", d)
    maps = lax.all_gather(mine, PLANE, axis=0, tiled=True)
    return scan_output(x, maps, act_here, dt_bias, decay_log, skip_gain, e)


def solution(mesh):
    spans, plane = mesh.devices.shape
    side = 4
    fine = Mesh(mesh.devices.reshape(spans // 2, 2, plane // side, side), ("z", "c", "x", "y"))
    placed = (
        P(("z", "c", "x", "y"), None),
        P(SPAN, PLANE, None, None, None),
        P(("z", "c", "x", "y"), None),
        P(("z", "c", "x", "y"), None),
        P(("z", "c", "x", "y"), None),
        P(),
        P(None, PLANE),
        P(None, PLANE),
        P(PLANE),
        P(PLANE, None),
        P(PLANE, None),
        P(PLANE),
        P(PLANE),
        P(PLANE),
    )
    return jax.shard_map(shards, mesh=fine, in_specs=placed, out_specs=P(SPAN, PLANE), check_vma=False)
```

time: 615 us -> 485 us (0.79)
  Pallas kernels: 0 us -> 132 us
  blocking collectives: 88.4 us -> 0 us
  waiting for transfers between devices: 314 us -> 247 us
  matrix products: 46.7 us -> 0 us
  local copies, waits for them, and re-layouts: 52.2 us -> 15.8 us
  other arithmetic: 41.4 us -> 13.4 us
  starting transfers between devices: 51.4 us -> 61 us
    all_gather x1 -> x2, waiting for transfers between devices: 204 us -> 21.3 us  [the longest x1 21.3 us: shards(): maps = lax.all_gather(mine, PLANE, axis=0, tiled=True)]
    pallas_call x0 -> x9, Pallas kernels: none -> 132 us  [the longest x4 68.4 us: project(): pl.pallas_call(project_body, name='project', grid=(shards, depth_steps),...]
    ppermute x8 -> x27, waiting for transfers between devices: 8.61 us -> 127 us  [the longest x19 124 us: shifted(): lax.ppermute(value, axis, [(i, (i + steps) % count) for i in range(count)])]
    psum x1 -> x0, blocking collectives: 88.4 us -> none  [shards(): state_proj, dt_raw = lax.psum((state_part, rate_part), 'exp')]
    dot_general x27 -> x0, matrix products: 44.9 us -> none  [the longest x1 23.8 us: shards(): jnp.dot(lax.all_gather(normed, 'exp', axis=0, tiled=True), in_weight, pre...]
    gather x2 -> x0, local copies, waits for them, and re-layouts: 20.2 us -> none  [shards(): picked = jnp.take(buffers, expert_ids * capacity + expert_slots, axis=0)]
    reshape x11 -> x0, local copies, waits for them, and re-layouts: 15.2 us -> none  [the longest x2 11.5 us: shards(): return output.astype(jnp.bfloat16).reshape(group_rows, local_width)]
    dynamic_update_slice x16 -> x0, other arithmetic: 11.2 us -> none  [shards(): lax.scan(advance, start_carry, (b_all.reshape(blocks, STRETCH, NSTATE), c...]
  transfers between devices with their start and end apart: 11 -> 30, of which waited for: 10 -> 12; matrix products, arithmetic and copies ran while one was open for 2% -> 4% of each run, Pallas kernels for 0% -> 10%
where the time goes in v1:
time: 485 us; the launch traced here: 483 us
  waiting for transfers between devices  247 us (51%)
  Pallas kernels  132 us (27%)
  starting transfers between devices  61 us (13%)
  local copies, waits for them, and re-layouts  15.8 us (3%)
  between operations  13.8 us (3%)
  other arithmetic  13.4 us (3%)
    ppermute x19, waiting for transfers between devices, shifted(): lax.ppermute(value, axis, [(i, (i + steps) % count) for i in range(count)])  124 us
    all_to_all x1, waiting for transfers between devices, shards(): lax.all_to_all(expert_rows, PLANE, split_axis=2, concat_axis=1, tiled=True)  98.7 us
    pallas_call x4, Pallas kernels, project(): pl.pallas_call(project_body, name='project', grid=(shards, depth_steps),...  68.4 us
    ppermute x19, starting transfers between devices, shifted(): lax.ppermute(value, axis, [(i, (i + steps) % count) for i in range(count)])  37.9 us
    all_gather x1, waiting for transfers between devices, shards(): maps = lax.all_gather(mine, PLANE, axis=0, tiled=True)  21.3 us
    pallas_call x1, Pallas kernels, scan_output(): pl.pallas_call(inside_body, name='inside', grid_spec=pltpu.PrefetchScalar...  19.5 us
    pallas_call x1, Pallas kernels, scan_output(): pl.pallas_call(state_body, name='states', grid_spec=pltpu.PrefetchScalarG...  18 us
    ppermute x8, starting transfers between devices, passed_on(): lax.ppermute(value, axes, [(i, i + steps) for i in range(count - steps)])  16.2 us
  transfers between devices with their start and end apart: 30, of which 12 were waited for; matrix products, arithmetic and copies ran while one was open for 4% of the time, Pallas kernels for 10%

profile of v1, /device:TPU:0, one launch (start us, length us, event | category | flops | bytes accessed | tf_op | source)
XLA Modules:
  0.0 483.1 jit_solution(15100911320345063112)
XLA Ops:
  7.8 1.6 collective-permute-start.4
  9.5 2.7 collective-permute-start.3
  12.2 1.4 collective-permute-start.2
  13.6 20.3 %collective-permute-done.4 = bf16[1024,512]{1,0:T(8,128)(2,1)S(1)} collective-permute-done((bf16[1024,512]{1,0:T(8,128)(2,1)S(1)}, bf16[1024,512]{1,0:T(8,128)(2,1)S(1)}, u32[]{:S(2)}, u32[]{:S(2)}) %collective-permute-start.4) | collective-permute-done | bytes 1048608 | tf_op jit(solution)/shard_map/ppermute | solution.py:23
  33.9 23.6 %collective-permute-done.3 = bf16[1024,512]{1,0:T(8,128)(2,1)S(1)} collective-permute-done((bf16[1024,512]{1,0:T(8,128)(2,1)S(1)}, bf16[1024,512]{1,0:T(8,128)(2,1)S(1)}, u32[]{:S(2)}, u32[]{:S(2)}) %collective-permute-start.3) | collective-permute-done | bytes 1048608 | tf_op jit(solution)/shard_map/ppermute | solution.py:23
  57.6 2.0 pad_maximum_fusion
  59.6 6.9 %all-to-all-start = ((bf16[1,1,16,24,8192]{4,3,1,0,2:T(8,128)(2,1)}), bf16[1,1,16,24,8192]{4,3,1,0,2:T(8,128)(2,1)}, u32[]{:S(2)}, u32[]{:S(2)}) async-start(bf16[1,1,16,24,8192]{4,3,1,0,2:T(8,128)(2,1)} %bitcast.69), calls=%async_computation | async-start | bytes 12582912 | tf_op jit(solution)/shard_map/all_to_all | solution.py:389
  68.0 98.7 %all-to-all-done = bf16[1,1,16,24,8192]{4,3,1,0,2:T(8,128)(2,1)} async-done(((bf16[1,1,16,24,8192]{4,3,1,0,2:T(8,128)(2,1)}), bf16[1,1,16,24,8192]{4,3,1,0,2:T(8,128)(2,1)}, u32[]{:S(2)}, u32[]{:S(2)}) %all-to-all-start) | async-done | bytes 6291488 | tf_op jit(solution)/shard_map/all_to_all | solution.py:389
  166.8 9.6 %combine.1.refs_0_ = bf16[128,8192]{1,0:T(8,128)(2,1)} custom-call(s32[128,2]{1,0:T(8,128)} %copy.42.index_ref, f32[128,2]{1,0:T(8,128)} %copy.43.weight_ref, bf16[384,8192]{1,0:T(8,128)(2,1)} %bitcast.3.rows_ref, bf16[128,8192]{1,0:T(8,128)(2,1)} %residual_ref.1, f32[1,8192]{1,0:T(1,128)} %bitcast.85), custom_call_target="tpu_custom_call" | custom-call | tf_op jit(solution)/shard_map/combine/pallas_call | solution.py:70
  176.4 3.2 collective-permute-start
  179.7 43.3 %collective-permute-done.1.refs_2_ = bf16[128,8192]{1,0:T(8,128)(2,1)S(1)} collective-permute-done((bf16[128,8192]{1,0:T(8,128)(2,1)}, bf16[128,8192]{1,0:T(8,128)(2,1)S(1)}, u32[]{:S(2)}, u32[]{:S(2)}) %collective-permute-start.1) | collective-permute-done | bytes 2097184 | tf_op jit(solution)/shard_map/ppermute | solution.py:23
  224.3 7.5 %collective-permute-start.9 = (f32[8,512]{1,0:T(8,128)S(1)}, f32[8,512]{1,0:T(8,128)S(1)}, u32[]{:S(2)}, u32[]{:S(2)}) collective-permute-start(f32[8,512]{1,0:T(8,128)S(1)} %get-tuple-element.32), channel_id=1, source_target_pairs={{0,8},{4,12},{8,0},{12,4},{1,9},{5,13},{9,1},{13,5},{2,10},{6,14},... | collective-permute-start | bytes 49160 | tf_op jit(solution)/shard_map/ppermute | solution.py:23
  231.8 2.5 collective-permute-start.8
  234.6 2.8 collective-permute-start.12
  237.3 4.0 collective-permute-start.11
  241.9 2.3 slice.111
  244.2 3.0 collective-permute-start.6
  247.2 2.2 pad_maximum_fusion.3.weight_ref
  249.4 11.2 %project.4 = bf16[1,3,128,512]{3,2,1,0:T(8,128)(2,1)} custom-call(bf16[128,8192]{1,0:T(8,128)(2,1)} %combine.1.refs_0_, bf16[128,8192]{1,0:T(8,128)(2,1)} %collective-permute-done.refs_1_, bf16[128,8192]{1,0:T(8,128)(2,1)} %copy-done, bf16[8192,512]{1,0:T(8,128)(2,1)} %refs_1_.1), custom_call_target="tpu_custom_call" | custom-call | tf_op jit(solution)/shard_map/project/pallas_call | solution.py:104
  260.6 2.9 collective-permute-done.6
  263.6 1.3 constant_dynamic-update-slice_fusion.refs_0_
  266.1 8.2 %project.6 = bf16[1,1,128,512]{3,2,1,0:T(8,128)(2,1)} custom-call(bf16[128,8192]{1,0:T(8,128)(2,1)} %copy-done.1, bf16[8192,512]{1,0:T(8,128)(2,1)} %refs_1_.1), custom_call_target="tpu_custom_call" | custom-call | tf_op jit(solution)/shard_map/project/pallas_call | solution.py:104
  274.4 21.8 %project.7 = bf16[3,1,128,512]{3,2,1,0:T(8,128)(2,1)} custom-call(bf16[128,8192]{1,0:T(8,128)(2,1)} %copy-done.1, bf16[8,3,1024,512]{3,2,1,0:T(8,128)(2,1)} %bitcast.67), custom_call_target="tpu_custom_call" | custom-call | tf_op jit(solution)/shard_map/project/pallas_call | solution.py:104
  296.2 27.2 %project.5 = bf16[3,3,128,512]{3,2,1,0:T(8,128)(2,1)} custom-call(bf16[128,8192]{1,0:T(8,128)(2,1)} %combine.1.refs_0_, bf16[128,8192]{1,0:T(8,128)(2,1)} %collective-permute-done.refs_1_, bf16[128,8192]{1,0:T(8,128)(2,1)} %copy-done, bf16[8,3,1024,512]{3,2,1,0:T(8,128)(2,1)} %bitcast.68), custom_call_target="tpu_custom_call" | custom-call | tf_op jit(solution)/shard_map/project/pallas_call | solution.py:104
  323.4 1.5 pad_maximum_fusion.1
  325.2 1.7 collective-permute-start.7
  327.8 1.4 copy.48.near_ref
  329.8 6.9 %filter.1 = (bf16[4,512,512]{2,1,0:T(8,128)(2,1)}, f32[512,256]{1,0:T(8,128)}) custom-call(s32[1]{0:T(128)} %bitcast.1.place_ref, bf16[4,3,128,512]{3,2,1,0:T(8,128)(2,1)} %copy.48.near_ref, bf16[4,1,128,512]{3,2,1,0:T(8,128)(2,1)} %fusion.far_ref, bf16[4,8,512]{2,1,0:T(8,128)(2,1)} %copy-done.8, f32[4,8,512]{2,1,0:T(8,128)} %pad_maximum_fusion.5.taps_ref, ...), custom_call_target="tpu_custom_call" | custom-call | tf_op jit(solution)/shard_map/filter/pallas_call | solution.py:150
  337.7 3.8 collective-permute-start.16
  342.4 4.8 collective-permute-done.16
  347.2 2.2 collective-permute-done.15
  350.6 1.6 fusion.9
  352.9 1.7 fusion.28
  354.5 3.1 collective-permute-start.19
  360.1 22.4 %collective-permute-done.19 = bf16[512,512]{1,0:T(8,128)(2,1)S(1)} collective-permute-done((bf16[512,512]{1,0:T(8,128)(2,1)S(1)}, bf16[512,512]{1,0:T(8,128)(2,1)S(1)}, u32[]{:S(2)}, u32[]{:S(2)}) %collective-permute-start.19) | collective-permute-done | bytes 524320 | tf_op jit(solution)/shard_map/ppermute | solution.py:23
  382.5 3.3 collective-permute-done.17
  385.9 1.6 pad_maximum_fusion.2.act_ref
  387.5 21.3 %all-gather.4.cloned.1.call-done.maps_ref = f32[2048,256]{1,0:T(8,128)} async-done(((f32[128,256]{1,0:T(8,128)}), f32[2048,256]{1,0:T(8,128)}) %all-gather.4.cloned.1.call-update) | async-done | bytes 2097168 | tf_op jit(solution)/shard_map/all_gather | solution.py:420
  408.7 18.0 %states.1 = (f32[8,64,512]{2,1,0:T(8,128)}, f32[2048,128]{1,0:T(8,128)}, f32[72,512]{1,0:T(8,128)}) custom-call(s32[1]{0:T(128)} %bitcast.place_ref, f32[2048,256]{1,0:T(8,128)} %all-gather.4.cloned.1.call-done.maps_ref, bf16[4,512,512]{2,1,0:T(8,128)(2,1)} %pad_maximum_fusion.2.act_ref, f32[128,128]{1,0:T(8,128)} %fusion.11.choice_ref, ...), custom_call_target="tpu_custom_call" | custom-call | tf_op jit(solution)/shard_map/states/pallas_call | solution.py:301
  426.7 4.9 %collective-permute-start.25 = (f32[72,512]{1,0:T(8,128)}, f32[72,512]{1,0:T(8,128)S(1)}, u32[]{:S(2)}, u32[]{:S(2)}) collective-permute-start(f32[72,512]{1,0:T(8,128)} %get-tuple-element.14), channel_id=1, source_target_pairs={{0,96},{16,112},{1,97},{17,113},{2,98},{18,114},{3,99},{19,115},{4... | collective-permute-start | bytes 442376 | tf_op jit(solution)/shard_map/ppermute | solution.py:28
  434.3 1.3 collective-permute-start.23
  435.6 1.3 collective-permute-start.22
  436.9 2.8 collective-permute-start.21
  439.7 1.7 collective-permute-start.20
  442.1 19.5 %inside.1.inside_ref = f32[2048,512]{1,0:T(8,128)} custom-call(s32[1]{0:T(128)} %bitcast.place_ref, f32[2048,256]{1,0:T(8,128)} %all-gather.4.cloned.1.call-done.maps_ref, bf16[4,512,512]{2,1,0:T(8,128)(2,1)} %pad_maximum_fusion.2.act_ref, f32[128,128]{1,0:T(8,128)} %fusion.11.choice_ref, f32[8,128]{1,0:T(8,128)} %fusion.23.choice_t_ref, ...), custom_call_target="tpu_custom_call" | custom-call | tf_op jit(solution)/shard_map/inside/pallas_call | solution.py:320
  461.6 1.3 collective-permute-start.26
  462.9 2.6 collective-permute-done.26
  466.3 9.9 %finish.1 = bf16[2048,512]{1,0:T(8,128)(2,1)} custom-call(f32[2048,512]{1,0:T(8,128)} %inside.1.inside_ref, f32[2048,256]{1,0:T(8,128)} %all-gather.4.cloned.1.call-done.maps_ref, f32[2048,128]{1,0:T(8,128)} %get-tuple-element.13.run_ref, f32[128,512]{1,0:T(8,128)} %fusion.1.spread_ref, f32[64,512]{1,0:T(8,128)} %fusion.2.entering_ref), custom_call_target="tpu_custom_call" | custom-call | tf_op jit(solution)/shard_map/finish/pallas_call | solution.py:348
  (103 shorter events, 18.6 us)
Async XLA Ops:
  6.5 267.8 %all-gather.6.cloned.1.call-start = ((), (), s32[]{:S(2)}) async-start(), calls=%async_computation.2 | async-start | bytes 28311552 | tf_op jit(solution)/shard_map/all_gather | solution.py:387
  7.8 26.1 %collective-permute-start.4 = (bf16[1024,512]{1,0:T(8,128)(2,1)S(1)}, bf16[1024,512]{1,0:T(8,128)(2,1)S(1)}, u32[]{:S(2)}, u32[]{:S(2)}) collective-permute-start(bf16[1024,512]{1,0:T(8,128)(2,1)S(1)} %constant_dynamic-slice_fusion), channel_id=1, source_target_pairs={{0,4},{4,8},{8,12},{12,0},{1,5},{5,9},{9,13},{13,1},{2,6},{6,10},{... | collective-permute-start | bytes 3145736 | tf_op jit(solution)/shard_map/ppermute | solution.py:23
  9.5 48.1 %collective-permute-start.3 = (bf16[1024,512]{1,0:T(8,128)(2,1)S(1)}, bf16[1024,512]{1,0:T(8,128)(2,1)S(1)}, u32[]{:S(2)}, u32[]{:S(2)}) collective-permute-start(bf16[1024,512]{1,0:T(8,128)(2,1)S(1)} %constant_dynamic-slice_fusion), channel_id=1, source_target_pairs={{0,8},{4,12},{8,0},{12,4},{1,9},{5,13},{9,1},{13,5},{2,10},{6,14},... | collective-permute-start | bytes 3145736 | tf_op jit(solution)/shard_map/ppermute | solution.py:23
  12.2 45.3 %collective-permute-start.2 = (bf16[1024,512]{1,0:T(8,128)(2,1)S(1)}, bf16[1024,512]{1,0:T(8,128)(2,1)S(1)}, u32[]{:S(2)}, u32[]{:S(2)}) collective-permute-start(bf16[1024,512]{1,0:T(8,128)(2,1)S(1)} %constant_dynamic-slice_fusion), channel_id=1, source_target_pairs={{0,12},{4,0},{8,4},{12,8},{1,13},{5,1},{9,5},{13,9},{2,14},{6,2},{... | collective-permute-start | bytes 3145736 | tf_op jit(solution)/shard_map/ppermute | solution.py:23
  59.6 7.0 %copy-start.12 = (s32[128,2]{0,1:T(2,128)S(1)}, s32[128,2]{0,1:T(2,128)}, u32[]{:S(2)}) copy-start(s32[128,2]{0,1:T(2,128)} %param.17) | copy-start | bytes 3076
  59.6 7.0 %copy-start.13 = (s32[128,2]{0,1:T(2,128)S(1)}, s32[128,2]{0,1:T(2,128)}, u32[]{:S(2)}) copy-start(s32[128,2]{0,1:T(2,128)} %param.16) | copy-start | bytes 3076
  59.6 7.7 %copy-start.11 = (f32[128,2]{0,1:T(2,128)S(1)}, f32[128,2]{0,1:T(2,128)}, u32[]{:S(2)}) copy-start(f32[128,2]{0,1:T(2,128)} %param.18) | copy-start | bytes 3076
  59.6 107.2 %all-to-all-start = ((bf16[1,1,16,24,8192]{4,3,1,0,2:T(8,128)(2,1)}), bf16[1,1,16,24,8192]{4,3,1,0,2:T(8,128)(2,1)}, u32[]{:S(2)}, u32[]{:S(2)}) async-start(bf16[1,1,16,24,8192]{4,3,1,0,2:T(8,128)(2,1)} %bitcast.69), calls=%async_computation | async-start | bytes 12582912 | tf_op jit(solution)/shard_map/all_to_all | solution.py:389
  66.5 342.2 %all-gather.4.cloned.1.call-start = ((), (), s32[]{:S(2)}) async-start(), calls=%async_computation.1 | async-start | bytes 2228224 | tf_op jit(solution)/shard_map/all_gather | solution.py:420
  176.3 47.8 %copy-start.9 = (f32[4,512]{1,0:T(4,128)S(1)}, f32[4,512]{1,0:T(4,128)}, u32[]{:S(2)}) copy-start(f32[4,512]{1,0:T(4,128)} %param.21) | copy-start | bytes 24580
  176.3 47.8 %copy-start.10 = (f32[512]{0:T(512)S(1)}, f32[512]{0:T(512)}, u32[]{:S(2)}) copy-start(f32[512]{0:T(512)} %param.22) | copy-start | bytes 6148
  176.4 58.0 %copy-start.6 = (bf16[512,128]{1,0:T(8,128)(2,1)S(1)}, bf16[512,128]{1,0:T(8,128)(2,1)}, u32[]{:S(2)}) copy-start(bf16[512,128]{1,0:T(8,128)(2,1)} %param.23) | copy-start | bytes 393220
  176.4 58.0 %copy-start.7 = (bf16[512,128]{1,0:T(8,128)(2,1)S(1)}, bf16[512,128]{1,0:T(8,128)(2,1)}, u32[]{:S(2)}) copy-start(bf16[512,128]{1,0:T(8,128)(2,1)} %param.24) | copy-start | bytes 393220
  176.4 46.6 %collective-permute-start.1 = (bf16[128,8192]{1,0:T(8,128)(2,1)}, bf16[128,8192]{1,0:T(8,128)(2,1)S(1)}, u32[]{:S(2)}, u32[]{:S(2)}) collective-permute-start(bf16[128,8192]{1,0:T(8,128)(2,1)} %combine.1.refs_0_), channel_id=1, source_target_pairs={{0,1},{1,2},{2,3},{3,0},{4,5},{5,6},{6,7},{7,4},{8,9},{9,10},{10,1... | collective-permute-start | bytes 6291464 | tf_op jit(solution)/shard_map/ppermute | solution.py:23
  176.4 65.5 %collective-permute-start = (bf16[128,8192]{1,0:T(8,128)(2,1)}, bf16[128,8192]{1,0:T(8,128)(2,1)}, u32[]{:S(2)}, u32[]{:S(2)}) collective-permute-start(bf16[128,8192]{1,0:T(8,128)(2,1)} %combine.1.refs_0_), channel_id=1, source_target_pairs={{0,3},{1,0},{2,1},{3,2},{4,7},{5,4},{6,5},{7,6},{8,11},{9,8},{10,9... | collective-permute-start | bytes 6291464 | tf_op jit(solution)/shard_map/ppermute | solution.py:23
  223.0 21.2 %copy-start = (bf16[128,8192]{1,0:T(8,128)(2,1)}, bf16[128,8192]{1,0:T(8,128)(2,1)S(1)}, u32[]{:S(2)}) copy-start(bf16[128,8192]{1,0:T(8,128)(2,1)S(1)} %collective-permute-done.1.refs_2_) | copy-start | bytes 6291460
  224.1 36.5 %collective-permute-start.5 = (bf16[64,8192]{1,0:T(8,128)(2,1)}, bf16[64,8192]{1,0:T(8,128)(2,1)S(1)}, u32[]{:S(2)}, u32[]{:S(2)}) collective-permute-start(bf16[64,8192]{1,0:T(8,128)(2,1)} %slice.110), channel_id=1, source_target_pairs={{0,1},{1,2},{2,3},{3,0},{4,5},{5,6},{6,7},{7,4},{8,9},{9,10},{10,1... | collective-permute-start | bytes 3145736 | tf_op jit(solution)/shard_map/ppermute | solution.py:23
  224.3 10.2 %collective-permute-start.10 = (f32[8,512]{1,0:T(8,128)S(1)}, f32[8,512]{1,0:T(8,128)S(1)}, u32[]{:S(2)}, u32[]{:S(2)}) collective-permute-start(f32[8,512]{1,0:T(8,128)S(1)} %get-tuple-element.32), channel_id=1, source_target_pairs={{0,4},{4,8},{8,12},{12,0},{1,5},{5,9},{9,13},{13,1},{2,6},{6,10},{... | collective-permute-start | bytes 49160 | tf_op jit(solution)/shard_map/ppermute | solution.py:23
  224.3 10.3 %collective-permute-start.9 = (f32[8,512]{1,0:T(8,128)S(1)}, f32[8,512]{1,0:T(8,128)S(1)}, u32[]{:S(2)}, u32[]{:S(2)}) collective-permute-start(f32[8,512]{1,0:T(8,128)S(1)} %get-tuple-element.32), channel_id=1, source_target_pairs={{0,8},{4,12},{8,0},{12,4},{1,9},{5,13},{9,1},{13,5},{2,10},{6,14},... | collective-permute-start | bytes 49160 | tf_op jit(solution)/shard_map/ppermute | solution.py:23
  231.8 5.5 %collective-permute-start.8 = (f32[8,512]{1,0:T(8,128)S(1)}, f32[8,512]{1,0:T(8,128)S(1)}, u32[]{:S(2)}, u32[]{:S(2)}) collective-permute-start(f32[8,512]{1,0:T(8,128)S(1)} %get-tuple-element.32), channel_id=1, source_target_pairs={{0,12},{4,0},{8,4},{12,8},{1,13},{5,1},{9,5},{13,9},{2,14},{6,2},{... | collective-permute-start | bytes 49160 | tf_op jit(solution)/shard_map/ppermute | solution.py:23
  234.5 12.7 %collective-permute-start.13 = (bf16[512,256]{1,0:T(8,128)(2,1)S(1)}, bf16[512,256]{1,0:T(8,128)(2,1)}, u32[]{:S(2)}, u32[]{:S(2)}) collective-permute-start(bf16[512,256]{1,0:T(8,128)(2,1)S(1)} %constant_dynamic-update-slice_fusion.2), channel_id=1, source_target_pairs={{0,4},{4,8},{8,12},{12,0},{1,5},{5,9},{9,13},{13,1},{2,6},{6,10},{... | collective-permute-start | bytes 786440 | tf_op jit(solution)/shard_map/ppermute | solution.py:23
  234.6 12.6 %collective-permute-start.12 = (bf16[512,256]{1,0:T(8,128)(2,1)S(1)}, bf16[512,256]{1,0:T(8,128)(2,1)}, u32[]{:S(2)}, u32[]{:S(2)}) collective-permute-start(bf16[512,256]{1,0:T(8,128)(2,1)S(1)} %constant_dynamic-update-slice_fusion.2), channel_id=1, source_target_pairs={{0,8},{4,12},{8,0},{12,4},{1,9},{5,13},{9,1},{13,5},{2,10},{6,14},... | collective-permute-start | bytes 786440 | tf_op jit(solution)/shard_map/ppermute | solution.py:23
  237.3 9.9 %collective-permute-start.11 = (bf16[512,256]{1,0:T(8,128)(2,1)S(1)}, bf16[512,256]{1,0:T(8,128)(2,1)}, u32[]{:S(2)}, u32[]{:S(2)}) collective-permute-start(bf16[512,256]{1,0:T(8,128)(2,1)S(1)} %constant_dynamic-update-slice_fusion.2), channel_id=1, source_target_pairs={{0,12},{4,0},{8,4},{12,8},{1,13},{5,1},{9,5},{13,9},{2,14},{6,2},{... | collective-permute-start | bytes 786440 | tf_op jit(solution)/shard_map/ppermute | solution.py:23
  244.2 19.4 %collective-permute-start.6 = (bf16[64,8192]{1,0:T(8,128)(2,1)}, bf16[64,8192]{1,0:T(8,128)(2,1)}, u32[]{:S(2)}, u32[]{:S(2)}) collective-permute-start(bf16[64,8192]{1,0:T(8,128)(2,1)} %slice.111), channel_id=1, source_target_pairs={{0,3},{1,0},{2,1},{3,2},{4,7},{5,4},{6,5},{7,6},{8,11},{9,8},{10,9... | collective-permute-start | bytes 3145736 | tf_op jit(solution)/shard_map/ppermute | solution.py:23
  264.9 1.3 copy-start.1
  296.2 27.2 %copy-start.3 = (bf16[1,3,128,512]{3,2,1,0:T(8,128)(2,1)S(1)}, bf16[1,3,128,512]{3,2,1,0:T(8,128)(2,1)}, u32[]{:S(2)}) copy-start(bf16[1,3,128,512]{3,2,1,0:T(8,128)(2,1)} %project.4) | copy-start | bytes 1179652
  323.4 1.6 copy-start.2
  323.4 1.7 copy-start.4
  323.4 1.7 copy-start.5
  325.2 3.9 collective-permute-start.7
  329.1 0.6 copy-start.8
  329.8 22.4 %copy-start.15 = (f32[8]{0:T(128)S(1)}, f32[8]{0:T(128)}, u32[]{:S(2)}) copy-start(f32[8]{0:T(128)} %param.26) | copy-start | bytes 100
  329.8 22.5 %copy-start.16 = (f32[8]{0:T(128)S(1)}, f32[8]{0:T(128)}, u32[]{:S(2)}) copy-start(f32[8]{0:T(128)} %param.25) | copy-start | bytes 100
  337.7 9.5 %collective-permute-start.16 = (f32[128,256]{1,0:T(8,128)S(1)}, f32[128,256]{1,0:T(8,128)S(1)}, u32[]{:S(2)}, u32[]{:S(2)}) collective-permute-start(f32[128,256]{1,0:T(8,128)S(1)} %get-tuple-element.28), channel_id=1, source_target_pairs={{0,3},{1,0},{2,1},{3,2},{4,7},{5,4},{6,5},{7,6},{8,11},{9,8},{10,9... | collective-permute-start | bytes 393224 | tf_op jit(solution)/shard_map/ppermute | solution.py:23
  341.4 7.9 %collective-permute-start.15 = (f32[128,256]{1,0:T(8,128)S(1)}, f32[128,256]{1,0:T(8,128)S(1)}, u32[]{:S(2)}, u32[]{:S(2)}) collective-permute-start(f32[128,256]{1,0:T(8,128)S(1)} %get-tuple-element.29), channel_id=1, source_target_pairs={{0,2},{1,3},{2,0},{3,1},{4,6},{5,7},{6,4},{7,5},{8,10},{9,11},{10,... | collective-permute-start | bytes 393224 | tf_op jit(solution)/shard_map/ppermute | solution.py:23
  341.5 9.1 %collective-permute-start.14 = (f32[128,256]{1,0:T(8,128)S(1)}, f32[128,256]{1,0:T(8,128)S(1)}, u32[]{:S(2)}, u32[]{:S(2)}) collective-permute-start(f32[128,256]{1,0:T(8,128)S(1)} %get-tuple-element.27), channel_id=1, source_target_pairs={{0,1},{1,2},{2,3},{3,0},{4,5},{5,6},{6,7},{7,4},{8,9},{9,10},{10,1... | collective-permute-start | bytes 393224 | tf_op jit(solution)/shard_map/ppermute | solution.py:23
  354.5 28.0 %collective-permute-start.19 = (bf16[512,512]{1,0:T(8,128)(2,1)S(1)}, bf16[512,512]{1,0:T(8,128)(2,1)S(1)}, u32[]{:S(2)}, u32[]{:S(2)}) collective-permute-start(bf16[512,512]{1,0:T(8,128)(2,1)S(1)} %get-tuple-element.21), channel_id=1, source_target_pairs={{0,12},{4,0},{8,4},{12,8},{1,13},{5,1},{9,5},{13,9},{2,14},{6,2},{... | collective-permute-start | bytes 1572872 | tf_op jit(solution)/shard_map/ppermute | solution.py:23
  357.6 25.0 %collective-permute-start.18 = (bf16[512,512]{1,0:T(8,128)(2,1)S(1)}, bf16[512,512]{1,0:T(8,128)(2,1)S(1)}, u32[]{:S(2)}, u32[]{:S(2)}) collective-permute-start(bf16[512,512]{1,0:T(8,128)(2,1)S(1)} %get-tuple-element.22), channel_id=1, source_target_pairs={{0,8},{4,12},{8,0},{12,4},{1,9},{5,13},{9,1},{13,5},{2,10},{6,14},... | collective-permute-start | bytes 1572872 | tf_op jit(solution)/shard_map/ppermute | solution.py:23
  357.6 28.3 %collective-permute-start.17 = (bf16[512,512]{1,0:T(8,128)(2,1)S(1)}, bf16[512,512]{1,0:T(8,128)(2,1)S(1)}, u32[]{:S(2)}, u32[]{:S(2)}) collective-permute-start(bf16[512,512]{1,0:T(8,128)(2,1)S(1)} %get-tuple-element.23), channel_id=1, source_target_pairs={{0,4},{4,8},{8,12},{12,0},{1,5},{5,9},{9,13},{13,1},{2,6},{6,10},{... | collective-permute-start | bytes 1572872 | tf_op jit(solution)/shard_map/ppermute | solution.py:23
  408.7 23.6 %copy-start.14 = (f32[8]{0:T(128)S(1)}, f32[8]{0:T(128)}, u32[]{:S(2)}) copy-start(f32[8]{0:T(128)} %param.27) | copy-start | bytes 100
  426.7 13.0 %collective-permute-start.25 = (f32[72,512]{1,0:T(8,128)}, f32[72,512]{1,0:T(8,128)S(1)}, u32[]{:S(2)}, u32[]{:S(2)}) collective-permute-start(f32[72,512]{1,0:T(8,128)} %get-tuple-element.14), channel_id=1, source_target_pairs={{0,96},{16,112},{1,97},{17,113},{2,98},{18,114},{3,99},{19,115},{4... | collective-permute-start | bytes 442376 | tf_op jit(solution)/shard_map/ppermute | solution.py:28
  433.0 28.5 %collective-permute-start.24 = (f32[72,512]{1,0:T(8,128)}, f32[72,512]{1,0:T(8,128)S(1)}, u32[]{:S(2)}, u32[]{:S(2)}) collective-permute-start(f32[72,512]{1,0:T(8,128)} %get-tuple-element.14), channel_id=1, source_target_pairs={{0,80},{16,96},{32,112},{1,81},{17,97},{33,113},{2,82},{18,98},{34... | collective-permute-start | bytes 442376 | tf_op jit(solution)/shard_map/ppermute | solution.py:28
  434.3 28.6 %collective-permute-start.23 = (f32[72,512]{1,0:T(8,128)}, f32[72,512]{1,0:T(8,128)S(1)}, u32[]{:S(2)}, u32[]{:S(2)}) collective-permute-start(f32[72,512]{1,0:T(8,128)} %get-tuple-element.14), channel_id=1, source_target_pairs={{0,64},{16,80},{32,96},{48,112},{1,65},{17,81},{33,97},{49,113},{2... | collective-permute-start | bytes 442376 | tf_op jit(solution)/shard_map/ppermute | solution.py:28
  435.6 27.3 %collective-permute-start.22 = (f32[72,512]{1,0:T(8,128)}, f32[72,512]{1,0:T(8,128)S(1)}, u32[]{:S(2)}, u32[]{:S(2)}) collective-permute-start(f32[72,512]{1,0:T(8,128)} %get-tuple-element.14), channel_id=1, source_target_pairs={{0,48},{16,64},{32,80},{48,96},{64,112},{1,49},{17,65},{33,81},{49... | collective-permute-start | bytes 442376 | tf_op jit(solution)/shard_map/ppermute | solution.py:28
  436.9 26.0 %collective-permute-start.21 = (f32[72,512]{1,0:T(8,128)}, f32[72,512]{1,0:T(8,128)S(1)}, u32[]{:S(2)}, u32[]{:S(2)}) collective-permute-start(f32[72,512]{1,0:T(8,128)} %get-tuple-element.14), channel_id=1, source_target_pairs={{0,32},{16,48},{32,64},{48,80},{64,96},{80,112},{1,33},{17,49},{33... | collective-permute-start | bytes 442376 | tf_op jit(solution)/shard_map/ppermute | solution.py:28
  439.7 23.2 %collective-permute-start.20 = (f32[72,512]{1,0:T(8,128)}, f32[72,512]{1,0:T(8,128)S(1)}, u32[]{:S(2)}, u32[]{:S(2)}) collective-permute-start(f32[72,512]{1,0:T(8,128)} %get-tuple-element.14), channel_id=1, source_target_pairs={{0,16},{16,32},{32,48},{48,64},{64,80},{80,96},{96,112},{1,17},{17... | collective-permute-start | bytes 442376 | tf_op jit(solution)/shard_map/ppermute | solution.py:28
  442.1 19.5 %copy-start.17 = (f32[72,512]{1,0:T(8,128)S(1)}, f32[72,512]{1,0:T(8,128)}, u32[]{:S(2)}) copy-start(f32[72,512]{1,0:T(8,128)} %get-tuple-element.14) | copy-start | bytes 442372
  461.6 4.0 collective-permute-start.26
Sparse Core Ops, SparseCore 0:
  59.7 122.3 all-gather.5
  352.3 56.3 all-gather.3

commit v2 on v1

--- a/solution.py
+++ b/solution.py
@@ -76,13 +76,14 @@
 
 
 def project_body(*refs):
-    *x_refs, w_ref, out_ref, acc_ref = refs
+    _, *x_refs, w_ref, out_ref, acc_ref = refs
     k = pl.program_id(1)
-    depth = w_ref.shape[-2]
+    weight = w_ref[...].reshape(-1, w_ref.shape[-1])
+    depth = weight.shape[0]
     rows = x_refs[0].shape[0]
     cols = pl.ds(pl.multiple_of(k * depth, depth), depth)
     left = jnp.concatenate([ref[:, cols] for ref in x_refs], axis=0)
-    part = dot(left, w_ref[...].reshape(w_ref.shape[-2:]))
+    part = dot(left, weight)
 
     @pl.when(k == 0)
     def _():
@@ -98,18 +99,21 @@
             out_ref[0, u] = acc_ref[u * rows : (u + 1) * rows].astype(BF16)
 
 
-def project(units, weight, weight_spec, shards, depth_steps):
+def project(place, units, weight, weight_spec, shards, depth_steps):
     rows, width = units[0].shape
     cols = weight.shape[-1]
     return pl.pallas_call(
         project_body,
         name="project",
-        grid=(shards, depth_steps),
-        in_specs=[whole((rows, width)) for _ in units] + [weight_spec],
-        out_specs=pl.BlockSpec((1, len(units), rows, cols), lambda r, k: (r, 0, 0, 0)),
+        grid_spec=pltpu.PrefetchScalarGridSpec(
+            num_scalar_prefetch=1,
+            grid=(shards, depth_steps),
+            in_specs=[whole((rows, width)) for _ in units] + [weight_spec],
+            out_specs=pl.BlockSpec((1, len(units), rows, cols), lambda r, k, _: (r, 0, 0, 0)),
+            scratch_shapes=[pltpu.VMEM((len(units) * rows, cols), F32)],
+        ),
         out_shape=jax.ShapeDtypeStruct((shards, len(units), rows, cols), BF16),
-        scratch_shapes=[pltpu.VMEM((len(units) * rows, cols), F32)],
-    )(*units, weight)
+    )(place.reshape(1), *units, weight)
 
 
 def filter_body(place_ref, near_ref, far_ref, rim_ref, taps_ref, weight_ref, act_ref, part_ref, pad_ref):
@@ -379,32 +383,36 @@
     depth = width // spans
 
     piece = lax.dynamic_slice_in_dim(in_weight, s * depth, depth, 0)
-    pieces = [shifted(piece, "x", -r) for r in range(1, nx)]
     maps_weight = jnp.concatenate([bc_weight, dt_weight], axis=1)
     taps = jnp.concatenate([conv_weight, conv_bias[None], jnp.zeros((7 - KCONV, local), F32)], axis=0)
     maps_weights = jnp.stack([maps_weight] + [shifted(maps_weight, "x", -r) for r in range(1, nx)])
     all_taps = jnp.stack([taps] + [shifted(taps, "x", -r) for r in range(1, nx)])
-    others = lax.all_gather(jnp.stack(pieces), SPAN)
+    everyone = lax.all_gather(piece, SPAN + ("x",)).reshape(spans, nx, depth, local)
 
     returned = lax.all_to_all(expert_rows, PLANE, split_axis=2, concat_axis=1, tiled=True)
+    returned, maps_weights, all_taps = lax.optimization_barrier((returned, maps_weights, all_taps))
     capacity = returned.shape[3]
     rows = returned.reshape(returned.shape[1] * capacity, width)
     normed = combine(expert_ids * capacity + expert_slots, combine_weights, rows, residual, norm_gain)
 
     below = shifted(normed, "y", 1)
     above = shifted(normed, "y", -1)
+    above, everyone = lax.optimization_barrier((above, everyone))
     half = own // 2
     far = jnp.concatenate([shifted(below[:half], "y", 1), shifted(above[half:], "y", -1)], axis=0)
 
-    own_spec = pl.BlockSpec((depth, local), lambda r, k: (k, 0))
-    other_spec = pl.BlockSpec((1, 1, depth, local), lambda r, k: (k, r, 0, 0))
-    near = (normed, above, below)
-    near_in = jnp.concatenate(
-        [project(near, in_weight, own_spec, 1, spans), project(near, others, other_spec, nx - 1, spans)], axis=0
-    )
-    far_in = jnp.concatenate(
-        [project((far,), in_weight, own_spec, 1, spans), project((far,), others, other_spec, nx - 1, spans)], axis=0
-    )
+    deep = 2
+    own_spec = pl.BlockSpec((deep * depth, local), lambda r, k, _: (k, 0))
+    other_spec = pl.BlockSpec((deep, 1, depth, local), lambda r, k, p: (k, (p[0] + r + 1) % nx, 0, 0))
+    steps = spans // deep
+
+    def projected(units):
+        here = project(x, units, in_weight, own_spec, 1, steps)
+        return jnp.concatenate([here, project(x, units, everyone, other_spec, nx - 1, steps)], axis=0)
+
+    near_in = projected((normed, above, below))
+    far, near_in = lax.optimization_barrier((far, near_in))
+    far_in = projected((far,))
 
     ends = jnp.stack([near_in[:, 0, -8:], near_in[:, 1, -8:], far_in[:, 0, -8:], near_in[:, 2, -8:]], axis=0)
     last = lax.dynamic_index_in_dim(ends, (ny - 1 - y) % ny, 0, keepdims=False)

time: 485 us -> 442 us (0.911)
  Pallas kernels: 132 us -> 115 us
  waiting for transfers between devices: 247 us -> 230 us
  starting transfers between devices: 61 us -> 52.7 us
    all_to_all x1, waiting for transfers between devices: 98.7 us -> 0.01 us  [shards(): lax.all_to_all(expert_rows, PLANE, split_axis=2, concat_axis=1, tiled=True)]
    ppermute x19 -> x16, waiting for transfers between devices: 124 us -> 207 us  [shifted(): lax.ppermute(value, axis, [(i, (i + steps) % count) for i in range(count)])]
    pallas_call x4, Pallas kernels: 68.4 us -> 51.3 us  [project(): pl.pallas_call(project_body, name='project', grid_spec=pltpu.PrefetchScal...]
    ppermute x19 -> x16, starting transfers between devices: 37.9 us -> 22.3 us  [shifted(): lax.ppermute(value, axis, [(i, (i + steps) % count) for i in range(count)])]
    ppermute x8, starting transfers between devices: 16.2 us -> 23 us  [passed_on(): lax.ppermute(value, axes, [(i, i + steps) for i in range(count - steps)])]
  transfers between devices with their start and end apart: 30 -> 27, of which waited for: 12 -> 10; matrix products, arithmetic and copies ran while one was open for 4% -> 4% of each run, Pallas kernels for 10% -> 13%
where the time goes in v2:
time: 442 us; the launch traced here: 441 us
  waiting for transfers between devices  230 us (52%)
  Pallas kernels  115 us (26%)
  starting transfers between devices  52.7 us (12%)
  other arithmetic  14.8 us (3%)
  between operations  13.8 us (3%)
  local copies, waits for them, and re-layouts  13.5 us (3%)
    ppermute x16, waiting for transfers between devices, shifted(): lax.ppermute(value, axis, [(i, (i + steps) % count) for i in range(count)])  207 us
    pallas_call x4, Pallas kernels, project(): pl.pallas_call(project_body, name='project', grid_spec=pltpu.PrefetchScal...  51.3 us
    ppermute x8, starting transfers between devices, passed_on(): lax.ppermute(value, axes, [(i, i + steps) for i in range(count - steps)])  23 us
    ppermute x16, starting transfers between devices, shifted(): lax.ppermute(value, axis, [(i, (i + steps) % count) for i in range(count)])  22.3 us
    all_gather x1, waiting for transfers between devices, shards(): maps = lax.all_gather(mine, PLANE, axis=0, tiled=True)  20.8 us
    pallas_call x1, Pallas kernels, scan_output(): pl.pallas_call(inside_body, name='inside', grid_spec=pltpu.PrefetchScalar...  19.5 us
    pallas_call x1, Pallas kernels, scan_output(): pl.pallas_call(state_body, name='states', grid_spec=pltpu.PrefetchScalarG...  18 us
    pallas_call x1, Pallas kernels, scan_output(): pl.pallas_call(finish_body, name='finish', grid=(blocks,), in_specs=[wide...  9.97 us
  transfers between devices with their start and end apart: 27, of which 10 were waited for; matrix products, arithmetic and copies ran while one was open for 4% of the time, Pallas kernels for 13%

profile of v2, /device:TPU:0, one launch (start us, length us, event | category | flops | bytes accessed | tf_op | source)
XLA Modules:
  0.0 440.5 jit_solution(15518949771678597472)
XLA Ops:
  6.5 2.3 constant_dynamic-slice_fusion
  8.9 7.3 %all-to-all-start = ((bf16[1,1,16,24,8192]{4,3,1,0,2:T(8,128)(2,1)}), bf16[1,1,16,24,8192]{4,3,1,0,2:T(8,128)(2,1)}, u32[]{:S(2)}, u32[]{:S(2)}) async-start(bf16[1,1,16,24,8192]{4,3,1,0,2:T(8,128)(2,1)} %bitcast.67), calls=%async_computation | async-start | bytes 12582912 | tf_op jit(solution)/shard_map/all_to_all | solution.py:392
  16.4 3.1 collective-permute-start.3
  19.6 0.9 collective-permute-start
  20.7 1.3 collective-permute-start.2
  22.0 3.9 collective-permute-start.4
  25.8 105.6 %collective-permute-done.3 = f32[8,512]{1,0:T(8,128)S(1)} collective-permute-done((f32[8,512]{1,0:T(8,128)S(1)}, f32[8,512]{1,0:T(8,128)S(1)}, u32[]{:S(2)}, u32[]{:S(2)}) %collective-permute-start.3) | collective-permute-done | bytes 16416 | tf_op jit(solution)/shard_map/ppermute | solution.py:23
  133.0 31.6 %collective-permute-done.4 = f32[8,512]{1,0:T(8,128)S(1)} collective-permute-done((f32[8,512]{1,0:T(8,128)S(1)}, f32[8,512]{1,0:T(8,128)S(1)}, u32[]{:S(2)}, u32[]{:S(2)}) %collective-permute-start.4) | collective-permute-done | bytes 16416 | tf_op jit(solution)/shard_map/ppermute | solution.py:23
  165.5 1.1 pad_maximum_fusion.3.weight_ref
  166.6 9.7 %combine.1.refs_1_ = bf16[128,8192]{1,0:T(8,128)(2,1)} custom-call(s32[128,2]{1,0:T(8,128)} %copy.42.index_ref, f32[128,2]{1,0:T(8,128)} %copy.43.weight_ref, bf16[384,8192]{1,0:T(8,128)(2,1)} %bitcast.13.rows_ref, bf16[128,8192]{1,0:T(8,128)(2,1)} %residual_ref.1, f32[1,8192]{1,0:T(1,128)} %bitcast.82), custom_call_target="tpu_custom_call" | custom-call | tf_op jit(solution)/shard_map/combine/pallas_call | solution.py:70
  176.3 1.2 collective-permute-start.6
  177.6 2.0 collective-permute-start.8
  179.6 42.8 %collective-permute-done.6.refs_3_ = bf16[128,8192]{1,0:T(8,128)(2,1)S(1)} collective-permute-done((bf16[128,8192]{1,0:T(8,128)(2,1)}, bf16[128,8192]{1,0:T(8,128)(2,1)S(1)}, u32[]{:S(2)}, u32[]{:S(2)}) %collective-permute-start.6) | collective-permute-done | bytes 2097184 | tf_op jit(solution)/shard_map/ppermute | solution.py:23
  222.5 2.8 slice.84
  225.3 2.6 collective-permute-start.9
  228.0 9.1 %project.4 = bf16[1,3,128,512]{3,2,1,0:T(8,128)(2,1)} custom-call(s32[1]{0:T(128)} %bitcast.refs_0_.place_ref, bf16[128,8192]{1,0:T(8,128)(2,1)} %combine.1.refs_1_, bf16[128,8192]{1,0:T(8,128)(2,1)} %collective-permute-done.8.refs_2_, bf16[128,8192]{1,0:T(8,128)(2,1)} %copy-done, bf16[8192,512]{1,0:T(8,128)(2,1)} %refs_2_.1), custom_call_target="tpu_custom_call" | custom-call | tf_op jit(solution)/shard_map/project/pallas_call | solution.py:105
  237.1 20.5 %project.5 = bf16[3,3,128,512]{3,2,1,0:T(8,128)(2,1)} custom-call(s32[1]{0:T(128)} %bitcast.refs_0_.place_ref, bf16[128,8192]{1,0:T(8,128)(2,1)} %combine.1.refs_1_, bf16[128,8192]{1,0:T(8,128)(2,1)} %collective-permute-done.8.refs_2_, bf16[128,8192]{1,0:T(8,128)(2,1)} %copy-done, bf16[8,4,1024,512]{3,2,1,0:T(8,128)(2,1)} %bitcast.65), custom_call_target="tpu_custom_call" | custom-call | tf_op jit(solution)/shard_map/project/pallas_call | solution.py:105
  257.6 1.4 pad_maximum_fusion.2
  259.0 3.0 pad_maximum_fusion.refs_1_
  262.1 15.4 %project.7 = bf16[3,1,128,512]{3,2,1,0:T(8,128)(2,1)} custom-call(s32[1]{0:T(128)} %bitcast.refs_0_.place_ref, bf16[128,8192]{1,0:T(8,128)(2,1)} %pad_maximum_fusion.refs_1_, bf16[8,4,1024,512]{3,2,1,0:T(8,128)(2,1)} %bitcast.66), custom_call_target="tpu_custom_call" | custom-call | tf_op jit(solution)/shard_map/project/pallas_call | solution.py:105
  277.5 6.3 %project.6 = bf16[1,1,128,512]{3,2,1,0:T(8,128)(2,1)} custom-call(s32[1]{0:T(128)} %bitcast.refs_0_.place_ref, bf16[128,8192]{1,0:T(8,128)(2,1)} %pad_maximum_fusion.refs_1_, bf16[8192,512]{1,0:T(8,128)(2,1)} %refs_2_.1), custom_call_target="tpu_custom_call" | custom-call | tf_op jit(solution)/shard_map/project/pallas_call | solution.py:105
  284.5 7.1 %collective-permute-start.10 = (bf16[4,8,512]{2,1,0:T(8,128)(2,1)S(1)}, bf16[4,8,512]{2,1,0:T(8,128)(2,1)S(1)}, u32[]{:S(2)}, u32[]{:S(2)}) collective-permute-start(bf16[4,8,512]{2,1,0:T(8,128)(2,1)S(1)} %pad_maximum_fusion.6), channel_id=1, source_target_pairs={{0,4},{4,8},{8,12},{12,16},{16,20},{20,24},{24,28},{28,32},{32,36}... | collective-permute-start | bytes 98312 | tf_op jit(solution)/shard_map/ppermute | solution.py:28
  291.6 1.7 fusion.far_ref
  293.4 1.3 copy.48.near_ref
  295.3 6.9 %filter.1 = (bf16[4,512,512]{2,1,0:T(8,128)(2,1)}, f32[512,256]{1,0:T(8,128)}) custom-call(s32[1]{0:T(128)} %bitcast.1.place_ref, bf16[4,3,128,512]{3,2,1,0:T(8,128)(2,1)} %copy.48.near_ref, bf16[4,1,128,512]{3,2,1,0:T(8,128)(2,1)} %fusion.far_ref, bf16[4,8,512]{2,1,0:T(8,128)(2,1)} %copy-done.5, f32[4,8,512]{2,1,0:T(8,128)} %pad_maximum_fusion.5.taps_ref, ...), custom_call_target="tpu_custom_call" | custom-call | tf_op jit(solution)/shard_map/filter/pallas_call | solution.py:154
  302.2 1.1 dynamic-slice_bitcast_fusion.2
  303.3 1.4 collective-permute-start.12
  304.8 1.8 collective-permute-start.13
  306.6 4.3 collective-permute-done.11
  311.8 1.6 fusion.9
  314.1 1.7 fusion.22
  316.6 1.6 collective-permute-start.15
  318.3 1.1 collective-permute-start.16
  320.8 9.7 %collective-permute-done.14 = bf16[512,512]{1,0:T(8,128)(2,1)S(1)} collective-permute-done((bf16[512,512]{1,0:T(8,128)(2,1)S(1)}, bf16[512,512]{1,0:T(8,128)(2,1)S(1)}, u32[]{:S(2)}, u32[]{:S(2)}) %collective-permute-start.14) | collective-permute-done | bytes 524320 | tf_op jit(solution)/shard_map/ppermute | solution.py:23
  330.5 11.8 %collective-permute-done.15 = bf16[512,512]{1,0:T(8,128)(2,1)S(1)} collective-permute-done((bf16[512,512]{1,0:T(8,128)(2,1)S(1)}, bf16[512,512]{1,0:T(8,128)(2,1)S(1)}, u32[]{:S(2)}, u32[]{:S(2)}) %collective-permute-start.15) | collective-permute-done | bytes 524320 | tf_op jit(solution)/shard_map/ppermute | solution.py:23
  342.3 1.6 pad_maximum_fusion.1.act_ref
  343.9 20.8 %all-gather.4.cloned.1.call-done.maps_ref = f32[2048,256]{1,0:T(8,128)} async-done(((f32[128,256]{1,0:T(8,128)}), f32[2048,256]{1,0:T(8,128)}) %all-gather.4.cloned.1.call-update) | async-done | bytes 2097168 | tf_op jit(solution)/shard_map/all_gather | solution.py:428
  364.7 18.0 %states.1 = (f32[8,64,512]{2,1,0:T(8,128)}, f32[2048,128]{1,0:T(8,128)}, f32[72,512]{1,0:T(8,128)}) custom-call(s32[1]{0:T(128)} %bitcast.refs_0_.place_ref, f32[2048,256]{1,0:T(8,128)} %all-gather.4.cloned.1.call-done.maps_ref, bf16[4,512,512]{2,1,0:T(8,128)(2,1)} %pad_maximum_fusion.1.act_ref, f32[128,128]{1,0:T(8,128)} %fusion.11.choice_ref, ...), custom_call_target="tpu_custom_call" | custom-call | tf_op jit(solution)/shard_map/states/pallas_call | solution.py:305
  382.7 1.3 collective-permute-start.17
  385.4 4.1 collective-permute-start.18
  389.5 4.2 collective-permute-start.19
  393.7 2.5 collective-permute-start.20
  396.2 1.3 collective-permute-start.21
  397.5 1.3 collective-permute-start.22
  399.5 19.5 %inside.1.inside_ref = f32[2048,512]{1,0:T(8,128)} custom-call(s32[1]{0:T(128)} %bitcast.refs_0_.place_ref, f32[2048,256]{1,0:T(8,128)} %all-gather.4.cloned.1.call-done.maps_ref, bf16[4,512,512]{2,1,0:T(8,128)(2,1)} %pad_maximum_fusion.1.act_ref, f32[128,128]{1,0:T(8,128)} %fusion.11.choice_ref, f32[8,128]{1,0:T(8,128)} %fusion.17.choice_t_ref, ...), custom_call_target="tpu_custom_call" | custom-call | tf_op jit(solution)/shard_map/inside/pallas_call | solution.py:324
  419.0 1.3 collective-permute-start.23
  420.4 2.6 collective-permute-done.23
  423.7 10.0 %finish.1 = bf16[2048,512]{1,0:T(8,128)(2,1)} custom-call(f32[2048,512]{1,0:T(8,128)} %inside.1.inside_ref, f32[2048,256]{1,0:T(8,128)} %all-gather.4.cloned.1.call-done.maps_ref, f32[2048,128]{1,0:T(8,128)} %get-tuple-element.27.run_ref, f32[128,512]{1,0:T(8,128)} %fusion.1.spread_ref, f32[64,512]{1,0:T(8,128)} %fusion.2.entering_ref), custom_call_target="tpu_custom_call" | custom-call | tf_op jit(solution)/shard_map/finish/pallas_call | solution.py:352
  (89 shorter events, 11.1 us)
Async XLA Ops:
  6.5 216.0 %all-gather.6.cloned.1.call-start = ((), (), s32[]{:S(2)}) async-start(), calls=%async_computation.2 | async-start | bytes 34603008 | tf_op jit(solution)/shard_map/all_gather | solution.py:390
  8.8 7.5 %copy-start.6 = (f32[4,512]{1,0:T(4,128)S(1)}, f32[4,512]{1,0:T(4,128)}, u32[]{:S(2)}) copy-start(f32[4,512]{1,0:T(4,128)} %param.21) | copy-start | bytes 24580
  8.8 7.5 %copy-start.7 = (f32[512]{0:T(512)S(1)}, f32[512]{0:T(512)}, u32[]{:S(2)}) copy-start(f32[512]{0:T(512)} %param.22) | copy-start | bytes 6148
  8.8 10.7 %copy-start.3 = (bf16[512,128]{1,0:T(8,128)(2,1)S(1)}, bf16[512,128]{1,0:T(8,128)(2,1)}, u32[]{:S(2)}) copy-start(bf16[512,128]{1,0:T(8,128)(2,1)} %param.23) | copy-start | bytes 393220
  8.9 10.7 %copy-start.4 = (bf16[512,128]{1,0:T(8,128)(2,1)S(1)}, bf16[512,128]{1,0:T(8,128)(2,1)}, u32[]{:S(2)}) copy-start(bf16[512,128]{1,0:T(8,128)(2,1)} %param.24) | copy-start | bytes 393220
  8.9 122.6 %copy-start.9 = (s32[128,2]{0,1:T(2,128)S(1)}, s32[128,2]{0,1:T(2,128)}, u32[]{:S(2)}) copy-start(s32[128,2]{0,1:T(2,128)} %param.17) | copy-start | bytes 3076
  8.9 122.6 %copy-start.10 = (s32[128,2]{0,1:T(2,128)S(1)}, s32[128,2]{0,1:T(2,128)}, u32[]{:S(2)}) copy-start(s32[128,2]{0,1:T(2,128)} %param.16) | copy-start | bytes 3076
  8.9 123.4 %copy-start.8 = (f32[128,2]{0,1:T(2,128)S(1)}, f32[128,2]{0,1:T(2,128)}, u32[]{:S(2)}) copy-start(f32[128,2]{0,1:T(2,128)} %param.18) | copy-start | bytes 3076
  8.9 157.7 %all-to-all-start = ((bf16[1,1,16,24,8192]{4,3,1,0,2:T(8,128)(2,1)}), bf16[1,1,16,24,8192]{4,3,1,0,2:T(8,128)(2,1)}, u32[]{:S(2)}, u32[]{:S(2)}) async-start(bf16[1,1,16,24,8192]{4,3,1,0,2:T(8,128)(2,1)} %bitcast.67), calls=%async_computation | async-start | bytes 12582912 | tf_op jit(solution)/shard_map/all_to_all | solution.py:392
  16.2 348.5 %all-gather.4.cloned.1.call-start = ((), (), s32[]{:S(2)}) async-start(), calls=%async_computation.1 | async-start | bytes 2228224 | tf_op jit(solution)/shard_map/all_gather | solution.py:428
  16.4 115.1 %collective-permute-start.3 = (f32[8,512]{1,0:T(8,128)S(1)}, f32[8,512]{1,0:T(8,128)S(1)}, u32[]{:S(2)}, u32[]{:S(2)}) collective-permute-start(f32[8,512]{1,0:T(8,128)S(1)} %get-tuple-element.46), channel_id=1, source_target_pairs={{0,12},{4,0},{8,4},{12,8},{1,13},{5,1},{9,5},{13,9},{2,14},{6,2},{... | collective-permute-start | bytes 49160 | tf_op jit(solution)/shard_map/ppermute | solution.py:23
  19.6 145.8 %collective-permute-start = (bf16[512,256]{1,0:T(8,128)(2,1)S(1)}, bf16[512,256]{1,0:T(8,128)(2,1)S(1)}, u32[]{:S(2)}, u32[]{:S(2)}) collective-permute-start(bf16[512,256]{1,0:T(8,128)(2,1)S(1)} %constant_dynamic-update-slice_fusion), channel_id=1, source_target_pairs={{0,12},{4,0},{8,4},{12,8},{1,13},{5,1},{9,5},{13,9},{2,14},{6,2},{... | collective-permute-start | bytes 786440 | tf_op jit(solution)/shard_map/ppermute | solution.py:23
  20.5 144.9 %collective-permute-start.1 = (bf16[512,256]{1,0:T(8,128)(2,1)S(1)}, bf16[512,256]{1,0:T(8,128)(2,1)S(1)}, u32[]{:S(2)}, u32[]{:S(2)}) collective-permute-start(bf16[512,256]{1,0:T(8,128)(2,1)S(1)} %constant_dynamic-update-slice_fusion), channel_id=1, source_target_pairs={{0,8},{4,12},{8,0},{12,4},{1,9},{5,13},{9,1},{13,5},{2,10},{6,14},... | collective-permute-start | bytes 786440 | tf_op jit(solution)/shard_map/ppermute | solution.py:23
  20.7 144.8 %collective-permute-start.2 = (bf16[512,256]{1,0:T(8,128)(2,1)S(1)}, bf16[512,256]{1,0:T(8,128)(2,1)S(1)}, u32[]{:S(2)}, u32[]{:S(2)}) collective-permute-start(bf16[512,256]{1,0:T(8,128)(2,1)S(1)} %constant_dynamic-update-slice_fusion), channel_id=1, source_target_pairs={{0,4},{4,8},{8,12},{12,0},{1,5},{5,9},{9,13},{13,1},{2,6},{6,10},{... | collective-permute-start | bytes 786440 | tf_op jit(solution)/shard_map/ppermute | solution.py:23
  22.0 142.6 %collective-permute-start.4 = (f32[8,512]{1,0:T(8,128)S(1)}, f32[8,512]{1,0:T(8,128)S(1)}, u32[]{:S(2)}, u32[]{:S(2)}) collective-permute-start(f32[8,512]{1,0:T(8,128)S(1)} %get-tuple-element.46), channel_id=1, source_target_pairs={{0,8},{4,12},{8,0},{12,4},{1,9},{5,13},{9,1},{13,5},{2,10},{6,14},... | collective-permute-start | bytes 49160 | tf_op jit(solution)/shard_map/ppermute | solution.py:23
  131.5 33.3 %collective-permute-start.5 = (f32[8,512]{1,0:T(8,128)S(1)}, f32[8,512]{1,0:T(8,128)S(1)}, u32[]{:S(2)}, u32[]{:S(2)}) collective-permute-start(f32[8,512]{1,0:T(8,128)S(1)} %get-tuple-element.46), channel_id=1, source_target_pairs={{0,4},{4,8},{8,12},{12,0},{1,5},{5,9},{9,13},{13,1},{2,6},{6,10},{... | collective-permute-start | bytes 49160 | tf_op jit(solution)/shard_map/ppermute | solution.py:23
  176.3 46.0 %collective-permute-start.6 = (bf16[128,8192]{1,0:T(8,128)(2,1)}, bf16[128,8192]{1,0:T(8,128)(2,1)S(1)}, u32[]{:S(2)}, u32[]{:S(2)}) collective-permute-start(bf16[128,8192]{1,0:T(8,128)(2,1)} %combine.1.refs_1_), channel_id=1, source_target_pairs={{0,1},{1,2},{2,3},{3,0},{4,5},{5,6},{6,7},{7,4},{8,9},{9,10},{10,1... | collective-permute-start | bytes 6291464 | tf_op jit(solution)/shard_map/ppermute | solution.py:23
  177.6 44.9 %collective-permute-start.8 = (bf16[128,8192]{1,0:T(8,128)(2,1)}, bf16[128,8192]{1,0:T(8,128)(2,1)}, u32[]{:S(2)}, u32[]{:S(2)}) collective-permute-start(bf16[128,8192]{1,0:T(8,128)(2,1)} %combine.1.refs_1_), channel_id=1, source_target_pairs={{0,3},{1,0},{2,1},{3,2},{4,7},{5,4},{6,5},{7,6},{8,11},{9,8},{10,9... | collective-permute-start | bytes 6291464 | tf_op jit(solution)/shard_map/ppermute | solution.py:23
  222.3 3.0 copy-start
  222.4 36.6 %collective-permute-start.7 = (bf16[64,8192]{1,0:T(8,128)(2,1)S(1)}, bf16[64,8192]{1,0:T(8,128)(2,1)}, u32[]{:S(2)}, u32[]{:S(2)}) collective-permute-start(bf16[64,8192]{1,0:T(8,128)(2,1)S(1)} %slice.110), channel_id=1, source_target_pairs={{0,1},{1,2},{2,3},{3,0},{4,5},{5,6},{6,7},{7,4},{8,9},{9,10},{10,1... | collective-permute-start | bytes 3145736 | tf_op jit(solution)/shard_map/ppermute | solution.py:23
  225.3 33.7 %collective-permute-start.9 = (bf16[64,8192]{1,0:T(8,128)(2,1)}, bf16[64,8192]{1,0:T(8,128)(2,1)}, u32[]{:S(2)}, u32[]{:S(2)}) collective-permute-start(bf16[64,8192]{1,0:T(8,128)(2,1)} %slice.84), channel_id=1, source_target_pairs={{0,3},{1,0},{2,1},{3,2},{4,7},{5,4},{6,5},{7,6},{8,11},{9,8},{10,9... | collective-permute-start | bytes 3145736 | tf_op jit(solution)/shard_map/ppermute | solution.py:23
  237.1 20.5 %copy-start.2 = (bf16[1,3,128,512]{3,2,1,0:T(8,128)(2,1)S(1)}, bf16[1,3,128,512]{3,2,1,0:T(8,128)(2,1)}, u32[]{:S(2)}) copy-start(bf16[1,3,128,512]{3,2,1,0:T(8,128)(2,1)} %project.4) | copy-start | bytes 1179652
  277.5 6.3 %copy-start.1 = (bf16[3,1,128,512]{3,2,1,0:T(8,128)(2,1)S(1)}, bf16[3,1,128,512]{3,2,1,0:T(8,128)(2,1)}, u32[]{:S(2)}) copy-start(bf16[3,1,128,512]{3,2,1,0:T(8,128)(2,1)} %project.7) | copy-start | bytes 1179652
  284.5 10.2 %collective-permute-start.10 = (bf16[4,8,512]{2,1,0:T(8,128)(2,1)S(1)}, bf16[4,8,512]{2,1,0:T(8,128)(2,1)S(1)}, u32[]{:S(2)}, u32[]{:S(2)}) collective-permute-start(bf16[4,8,512]{2,1,0:T(8,128)(2,1)S(1)} %pad_maximum_fusion.6), channel_id=1, source_target_pairs={{0,4},{4,8},{8,12},{12,16},{16,20},{20,24},{24,28},{28,32},{32,36}... | collective-permute-start | bytes 98312 | tf_op jit(solution)/shard_map/ppermute | solution.py:28
  294.7 0.6 copy-start.5
  295.3 18.1 %copy-start.12 = (f32[8]{0:T(128)S(1)}, f32[8]{0:T(128)}, u32[]{:S(2)}) copy-start(f32[8]{0:T(128)} %param.26) | copy-start | bytes 100
  295.3 18.1 %copy-start.13 = (f32[8]{0:T(128)S(1)}, f32[8]{0:T(128)}, u32[]{:S(2)}) copy-start(f32[8]{0:T(128)} %param.25) | copy-start | bytes 100
  303.3 7.7 %collective-permute-start.11 = (f32[128,256]{1,0:T(8,128)S(1)}, f32[128,256]{1,0:T(8,128)S(1)}, u32[]{:S(2)}, u32[]{:S(2)}) collective-permute-start(f32[128,256]{1,0:T(8,128)S(1)} %get-tuple-element.41), channel_id=1, source_target_pairs={{0,1},{1,2},{2,3},{3,0},{4,5},{5,6},{6,7},{7,4},{8,9},{9,10},{10,1... | collective-permute-start | bytes 393224 | tf_op jit(solution)/shard_map/ppermute | solution.py:23
  303.3 7.6 %collective-permute-start.12 = (f32[128,256]{1,0:T(8,128)S(1)}, f32[128,256]{1,0:T(8,128)S(1)}, u32[]{:S(2)}, u32[]{:S(2)}) collective-permute-start(f32[128,256]{1,0:T(8,128)S(1)} %get-tuple-element.43), channel_id=1, source_target_pairs={{0,2},{1,3},{2,0},{3,1},{4,6},{5,7},{6,4},{7,5},{8,10},{9,11},{10,... | collective-permute-start | bytes 393224 | tf_op jit(solution)/shard_map/ppermute | solution.py:23
  304.8 7.0 %collective-permute-start.13 = (f32[128,256]{1,0:T(8,128)S(1)}, f32[128,256]{1,0:T(8,128)S(1)}, u32[]{:S(2)}, u32[]{:S(2)}) collective-permute-start(f32[128,256]{1,0:T(8,128)S(1)} %get-tuple-element.42), channel_id=1, source_target_pairs={{0,3},{1,0},{2,1},{3,2},{4,7},{5,4},{6,5},{7,6},{8,11},{9,8},{10,9... | collective-permute-start | bytes 393224 | tf_op jit(solution)/shard_map/ppermute | solution.py:23
  315.8 14.8 %collective-permute-start.14 = (bf16[512,512]{1,0:T(8,128)(2,1)S(1)}, bf16[512,512]{1,0:T(8,128)(2,1)S(1)}, u32[]{:S(2)}, u32[]{:S(2)}) collective-permute-start(bf16[512,512]{1,0:T(8,128)(2,1)S(1)} %get-tuple-element.37), channel_id=1, source_target_pairs={{0,4},{4,8},{8,12},{12,0},{1,5},{5,9},{9,13},{13,1},{2,6},{6,10},{... | collective-permute-start | bytes 1572872 | tf_op jit(solution)/shard_map/ppermute | solution.py:23
  316.6 25.7 %collective-permute-start.15 = (bf16[512,512]{1,0:T(8,128)(2,1)S(1)}, bf16[512,512]{1,0:T(8,128)(2,1)S(1)}, u32[]{:S(2)}, u32[]{:S(2)}) collective-permute-start(bf16[512,512]{1,0:T(8,128)(2,1)S(1)} %get-tuple-element.36), channel_id=1, source_target_pairs={{0,8},{4,12},{8,0},{12,4},{1,9},{5,13},{9,1},{13,5},{2,10},{6,14},... | collective-permute-start | bytes 1572872 | tf_op jit(solution)/shard_map/ppermute | solution.py:23
  318.3 24.0 %collective-permute-start.16 = (bf16[512,512]{1,0:T(8,128)(2,1)S(1)}, bf16[512,512]{1,0:T(8,128)(2,1)S(1)}, u32[]{:S(2)}, u32[]{:S(2)}) collective-permute-start(bf16[512,512]{1,0:T(8,128)(2,1)S(1)} %get-tuple-element.35), channel_id=1, source_target_pairs={{0,12},{4,0},{8,4},{12,8},{1,13},{5,1},{9,5},{13,9},{2,14},{6,2},{... | collective-permute-start | bytes 1572872 | tf_op jit(solution)/shard_map/ppermute | solution.py:23
  343.9 40.8 %copy-start.11 = (f32[8]{0:T(128)S(1)}, f32[8]{0:T(128)}, u32[]{:S(2)}) copy-start(f32[8]{0:T(128)} %param.27) | copy-start | bytes 100
  382.7 14.8 %collective-permute-start.17 = (f32[72,512]{1,0:T(8,128)}, f32[72,512]{1,0:T(8,128)S(1)}, u32[]{:S(2)}, u32[]{:S(2)}) collective-permute-start(f32[72,512]{1,0:T(8,128)} %get-tuple-element.28), channel_id=1, source_target_pairs={{0,16},{16,32},{32,48},{48,64},{64,80},{80,96},{96,112},{1,17},{17... | collective-permute-start | bytes 442376 | tf_op jit(solution)/shard_map/ppermute | solution.py:28
  385.4 33.6 %collective-permute-start.18 = (f32[72,512]{1,0:T(8,128)}, f32[72,512]{1,0:T(8,128)S(1)}, u32[]{:S(2)}, u32[]{:S(2)}) collective-permute-start(f32[72,512]{1,0:T(8,128)} %get-tuple-element.28), channel_id=1, source_target_pairs={{0,32},{16,48},{32,64},{48,80},{64,96},{80,112},{1,33},{17,49},{33... | collective-permute-start | bytes 442376 | tf_op jit(solution)/shard_map/ppermute | solution.py:28
  389.5 30.8 %collective-permute-start.19 = (f32[72,512]{1,0:T(8,128)}, f32[72,512]{1,0:T(8,128)S(1)}, u32[]{:S(2)}, u32[]{:S(2)}) collective-permute-start(f32[72,512]{1,0:T(8,128)} %get-tuple-element.28), channel_id=1, source_target_pairs={{0,48},{16,64},{32,80},{48,96},{64,112},{1,49},{17,65},{33,81},{49... | collective-permute-start | bytes 442376 | tf_op jit(solution)/shard_map/ppermute | solution.py:28
  393.7 26.7 %collective-permute-start.20 = (f32[72,512]{1,0:T(8,128)}, f32[72,512]{1,0:T(8,128)S(1)}, u32[]{:S(2)}, u32[]{:S(2)}) collective-permute-start(f32[72,512]{1,0:T(8,128)} %get-tuple-element.28), channel_id=1, source_target_pairs={{0,64},{16,80},{32,96},{48,112},{1,65},{17,81},{33,97},{49,113},{2... | collective-permute-start | bytes 442376 | tf_op jit(solution)/shard_map/ppermute | solution.py:28
  396.2 24.1 %collective-permute-start.21 = (f32[72,512]{1,0:T(8,128)}, f32[72,512]{1,0:T(8,128)S(1)}, u32[]{:S(2)}, u32[]{:S(2)}) collective-permute-start(f32[72,512]{1,0:T(8,128)} %get-tuple-element.28), channel_id=1, source_target_pairs={{0,80},{16,96},{32,112},{1,81},{17,97},{33,113},{2,82},{18,98},{34... | collective-permute-start | bytes 442376 | tf_op jit(solution)/shard_map/ppermute | solution.py:28
  397.5 22.8 %collective-permute-start.22 = (f32[72,512]{1,0:T(8,128)}, f32[72,512]{1,0:T(8,128)S(1)}, u32[]{:S(2)}, u32[]{:S(2)}) collective-permute-start(f32[72,512]{1,0:T(8,128)} %get-tuple-element.28), channel_id=1, source_target_pairs={{0,96},{16,112},{1,97},{17,113},{2,98},{18,114},{3,99},{19,115},{4... | collective-permute-start | bytes 442376 | tf_op jit(solution)/shard_map/ppermute | solution.py:28
  399.5 19.5 %copy-start.14 = (f32[72,512]{1,0:T(8,128)S(1)}, f32[72,512]{1,0:T(8,128)}, u32[]{:S(2)}) copy-start(f32[72,512]{1,0:T(8,128)} %get-tuple-element.28) | copy-start | bytes 442372
  419.0 4.0 collective-permute-start.23
Sparse Core Ops, SparseCore 0:
  9.6 188.4 all-gather.5
  313.5 51.1 all-gather.3

commit v3 on v2

--- a/solution.py
+++ b/solution.py
@@ -385,19 +385,19 @@
     piece = lax.dynamic_slice_in_dim(in_weight, s * depth, depth, 0)
     maps_weight = jnp.concatenate([bc_weight, dt_weight], axis=1)
     taps = jnp.concatenate([conv_weight, conv_bias[None], jnp.zeros((7 - KCONV, local), F32)], axis=0)
-    maps_weights = jnp.stack([maps_weight] + [shifted(maps_weight, "x", -r) for r in range(1, nx)])
-    all_taps = jnp.stack([taps] + [shifted(taps, "x", -r) for r in range(1, nx)])
     everyone = lax.all_gather(piece, SPAN + ("x",)).reshape(spans, nx, depth, local)
 
     returned = lax.all_to_all(expert_rows, PLANE, split_axis=2, concat_axis=1, tiled=True)
-    returned, maps_weights, all_taps = lax.optimization_barrier((returned, maps_weights, all_taps))
     capacity = returned.shape[3]
     rows = returned.reshape(returned.shape[1] * capacity, width)
     normed = combine(expert_ids * capacity + expert_slots, combine_weights, rows, residual, norm_gain)
 
     below = shifted(normed, "y", 1)
     above = shifted(normed, "y", -1)
-    above, everyone = lax.optimization_barrier((above, everyone))
+    maps_weight, taps, _ = lax.optimization_barrier((maps_weight, taps, normed))
+    maps_weights = jnp.stack([maps_weight] + [shifted(maps_weight, "x", -r) for r in range(1, nx)])
+    all_taps = jnp.stack([taps] + [shifted(taps, "x", -r) for r in range(1, nx)])
+    above, everyone, maps_weights, all_taps = lax.optimization_barrier((above, everyone, maps_weights, all_taps))
     half = own // 2
     far = jnp.concatenate([shifted(below[:half], "y", 1), shifted(above[half:], "y", -1)], axis=0)
 

time: 442 us -> 418 us (0.946)
  waiting for transfers between devices: 230 us -> 206 us
    ppermute x16, waiting for transfers between devices: 207 us -> 57 us  [shifted(): lax.ppermute(value, axis, [(i, (i + steps) % count) for i in range(count)])]
    all_to_all x1, waiting for transfers between devices: 0.01 us -> 123 us  [shards(): lax.all_to_all(expert_rows, PLANE, split_axis=2, concat_axis=1, tiled=True)]
  transfers between devices with their start and end apart: 27 -> 27, of which waited for: 10 -> 14; matrix products, arithmetic and copies ran while one was open for 4% -> 4% of each run, Pallas kernels for 13% -> 14%
where the time goes in v3:
time: 418 us; the launch traced here: 416 us
  waiting for transfers between devices  206 us (49%)
  Pallas kernels  115 us (28%)
  starting transfers between devices  53.7 us (13%)
  other arithmetic  14.9 us (4%)
  between operations  13.7 us (3%)
  local copies, waits for them, and re-layouts  12.9 us (3%)
    all_to_all x1, waiting for transfers between devices, shards(): lax.all_to_all(expert_rows, PLANE, split_axis=2, concat_axis=1, tiled=True)  123 us
    ppermute x16, waiting for transfers between devices, shifted(): lax.ppermute(value, axis, [(i, (i + steps) % count) for i in range(count)])  57 us
    pallas_call x4, Pallas kernels, project(): pl.pallas_call(project_body, name='project', grid_spec=pltpu.PrefetchScal...  51.3 us
    ppermute x16, starting transfers between devices, shifted(): lax.ppermute(value, axis, [(i, (i + steps) % count) for i in range(count)])  25.9 us
    all_gather x1, waiting for transfers between devices, shards(): maps = lax.all_gather(mine, PLANE, axis=0, tiled=True)  22.1 us
    ppermute x8, starting transfers between devices, passed_on(): lax.ppermute(value, axes, [(i, i + steps) for i in range(count - steps)])  20.4 us
    pallas_call x1, Pallas kernels, scan_output(): pl.pallas_call(inside_body, name='inside', grid_spec=pltpu.PrefetchScalar...  19.4 us
    pallas_call x1, Pallas kernels, scan_output(): pl.pallas_call(state_body, name='states', grid_spec=pltpu.PrefetchScalarG...  18 us
  transfers between devices with their start and end apart: 27, of which 14 were waited for; matrix products, arithmetic and copies ran while one was open for 4% of the time, Pallas kernels for 14%

profile of v3, /device:TPU:0, one launch (start us, length us, event | category | flops | bytes accessed | tf_op | source)
XLA Modules:
  0.0 416.4 jit_solution(13154696988586303448)
XLA Ops:
  6.5 2.3 constant_dynamic-slice_fusion
  8.9 7.3 %all-to-all-start = ((bf16[1,1,16,24,8192]{4,3,1,0,2:T(8,128)(2,1)}), bf16[1,1,16,24,8192]{4,3,1,0,2:T(8,128)(2,1)}, u32[]{:S(2)}, u32[]{:S(2)}) async-start(bf16[1,1,16,24,8192]{4,3,1,0,2:T(8,128)(2,1)} %bitcast.65), calls=%async_computation | async-start | bytes 12582912 | tf_op jit(solution)/shard_map/all_to_all | solution.py:390
  17.8 123.3 %all-to-all-done = bf16[1,1,16,24,8192]{4,3,1,0,2:T(8,128)(2,1)} async-done(((bf16[1,1,16,24,8192]{4,3,1,0,2:T(8,128)(2,1)}), bf16[1,1,16,24,8192]{4,3,1,0,2:T(8,128)(2,1)}, u32[]{:S(2)}, u32[]{:S(2)}) %all-to-all-start) | async-done | bytes 6291488 | tf_op jit(solution)/shard_map/all_to_all | solution.py:390
  141.0 9.9 %combine.1.refs_1_ = bf16[128,8192]{1,0:T(8,128)(2,1)} custom-call(s32[128,2]{1,0:T(8,128)} %copy.42.index_ref, f32[128,2]{1,0:T(8,128)} %copy.43.weight_ref, bf16[384,8192]{1,0:T(8,128)(2,1)} %bitcast.3.rows_ref, bf16[128,8192]{1,0:T(8,128)(2,1)} %residual_ref.1, f32[1,8192]{1,0:T(1,128)} %bitcast.81), custom_call_target="tpu_custom_call" | custom-call | tf_op jit(solution)/shard_map/combine/pallas_call | solution.py:70
  151.1 3.1 collective-permute-start.2
  154.4 3.4 collective-permute-start.6
  157.8 1.8 collective-permute-start.7
  159.6 1.3 collective-permute-start.8
  161.7 1.8 collective-permute-done.7
  163.5 2.3 collective-permute-start.3
  166.5 10.2 %collective-permute-done.5 = bf16[512,256]{1,0:T(8,128)(2,1)S(1)} collective-permute-done((bf16[512,256]{1,0:T(8,128)(2,1)S(1)}, bf16[512,256]{1,0:T(8,128)(2,1)S(1)}, u32[]{:S(2)}, u32[]{:S(2)}) %collective-permute-start.5) | collective-permute-done | bytes 262176 | tf_op jit(solution)/shard_map/ppermute | solution.py:23
  176.7 1.5 collective-permute-done.3
  178.2 8.2 %collective-permute-done.4 = bf16[512,256]{1,0:T(8,128)(2,1)S(1)} collective-permute-done((bf16[512,256]{1,0:T(8,128)(2,1)S(1)}, bf16[512,256]{1,0:T(8,128)(2,1)S(1)}, u32[]{:S(2)}, u32[]{:S(2)}) %collective-permute-start.4) | collective-permute-done | bytes 262176 | tf_op jit(solution)/shard_map/ppermute | solution.py:23
  187.5 9.1 %collective-permute-done.refs_3_ = bf16[128,8192]{1,0:T(8,128)(2,1)S(1)} collective-permute-done((bf16[128,8192]{1,0:T(8,128)(2,1)}, bf16[128,8192]{1,0:T(8,128)(2,1)S(1)}, u32[]{:S(2)}, u32[]{:S(2)}) %collective-permute-start) | collective-permute-done | bytes 2097184 | tf_op jit(solution)/shard_map/ppermute | solution.py:23
  198.1 2.3 slice.84
  200.4 2.0 collective-permute-start.9
  202.4 9.1 %project.4 = bf16[1,3,128,512]{3,2,1,0:T(8,128)(2,1)} custom-call(s32[1]{0:T(128)} %bitcast.refs_0_.place_ref, bf16[128,8192]{1,0:T(8,128)(2,1)} %combine.1.refs_1_, bf16[128,8192]{1,0:T(8,128)(2,1)} %collective-permute-done.2.refs_2_, bf16[128,8192]{1,0:T(8,128)(2,1)} %copy-done, bf16[8192,512]{1,0:T(8,128)(2,1)} %refs_2_.1), custom_call_target="tpu_custom_call" | custom-call | tf_op jit(solution)/shard_map/project/pallas_call | solution.py:105
  211.5 20.5 %project.5 = bf16[3,3,128,512]{3,2,1,0:T(8,128)(2,1)} custom-call(s32[1]{0:T(128)} %bitcast.refs_0_.place_ref, bf16[128,8192]{1,0:T(8,128)(2,1)} %combine.1.refs_1_, bf16[128,8192]{1,0:T(8,128)(2,1)} %collective-permute-done.2.refs_2_, bf16[128,8192]{1,0:T(8,128)(2,1)} %copy-done, bf16[8,4,1024,512]{3,2,1,0:T(8,128)(2,1)} %bitcast.63), custom_call_target="tpu_custom_call" | custom-call | tf_op jit(solution)/shard_map/project/pallas_call | solution.py:105
  232.0 1.4 pad_maximum_fusion.2
  233.4 3.0 pad_maximum_fusion.refs_1_
  236.5 15.4 %project.7 = bf16[3,1,128,512]{3,2,1,0:T(8,128)(2,1)} custom-call(s32[1]{0:T(128)} %bitcast.refs_0_.place_ref, bf16[128,8192]{1,0:T(8,128)(2,1)} %pad_maximum_fusion.refs_1_, bf16[8,4,1024,512]{3,2,1,0:T(8,128)(2,1)} %bitcast.64), custom_call_target="tpu_custom_call" | custom-call | tf_op jit(solution)/shard_map/project/pallas_call | solution.py:105
  251.9 6.3 %project.6 = bf16[1,1,128,512]{3,2,1,0:T(8,128)(2,1)} custom-call(s32[1]{0:T(128)} %bitcast.refs_0_.place_ref, bf16[128,8192]{1,0:T(8,128)(2,1)} %pad_maximum_fusion.refs_1_, bf16[8192,512]{1,0:T(8,128)(2,1)} %refs_2_.1), custom_call_target="tpu_custom_call" | custom-call | tf_op jit(solution)/shard_map/project/pallas_call | solution.py:105
  259.0 4.5 %collective-permute-start.10 = (bf16[4,8,512]{2,1,0:T(8,128)(2,1)S(1)}, bf16[4,8,512]{2,1,0:T(8,128)(2,1)S(1)}, u32[]{:S(2)}, u32[]{:S(2)}) collective-permute-start(bf16[4,8,512]{2,1,0:T(8,128)(2,1)S(1)} %pad_maximum_fusion.7), channel_id=1, source_target_pairs={{0,4},{4,8},{8,12},{12,16},{16,20},{20,24},{24,28},{28,32},{32,36}... | collective-permute-start | bytes 98312 | tf_op jit(solution)/shard_map/ppermute | solution.py:28
  263.4 1.7 fusion.far_ref
  265.2 1.4 copy.48.near_ref
  267.1 6.8 %filter.1 = (bf16[4,512,512]{2,1,0:T(8,128)(2,1)}, f32[512,256]{1,0:T(8,128)}) custom-call(s32[1]{0:T(128)} %bitcast.1.place_ref, bf16[4,3,128,512]{3,2,1,0:T(8,128)(2,1)} %copy.48.near_ref, bf16[4,1,128,512]{3,2,1,0:T(8,128)(2,1)} %fusion.far_ref, bf16[4,8,512]{2,1,0:T(8,128)(2,1)} %copy-done.5, f32[4,8,512]{2,1,0:T(8,128)} %pad_maximum_fusion.6.taps_ref, ...), custom_call_target="tpu_custom_call" | custom-call | tf_op jit(solution)/shard_map/filter/pallas_call | solution.py:154
  275.1 2.1 collective-permute-start.11
  277.8 2.5 collective-permute-start.13
  280.3 4.2 %collective-permute-done.11 = f32[128,256]{1,0:T(8,128)S(1)} collective-permute-done((f32[128,256]{1,0:T(8,128)S(1)}, f32[128,256]{1,0:T(8,128)S(1)}, u32[]{:S(2)}, u32[]{:S(2)}) %collective-permute-start.11) | collective-permute-done | bytes 131104 | tf_op jit(solution)/shard_map/ppermute | solution.py:23
  285.1 1.6 fusion.9
  287.4 1.7 fusion.21
  289.0 1.7 collective-permute-start.14
  290.7 2.0 collective-permute-start.15
  292.7 1.4 collective-permute-start.16
  295.6 10.8 %collective-permute-done.14 = bf16[512,512]{1,0:T(8,128)(2,1)S(1)} collective-permute-done((bf16[512,512]{1,0:T(8,128)(2,1)S(1)}, bf16[512,512]{1,0:T(8,128)(2,1)S(1)}, u32[]{:S(2)}, u32[]{:S(2)}) %collective-permute-start.14) | collective-permute-done | bytes 524320 | tf_op jit(solution)/shard_map/ppermute | solution.py:23
  306.4 10.0 %collective-permute-done.15 = bf16[512,512]{1,0:T(8,128)(2,1)S(1)} collective-permute-done((bf16[512,512]{1,0:T(8,128)(2,1)S(1)}, bf16[512,512]{1,0:T(8,128)(2,1)S(1)}, u32[]{:S(2)}, u32[]{:S(2)}) %collective-permute-start.15) | collective-permute-done | bytes 524320 | tf_op jit(solution)/shard_map/ppermute | solution.py:23
  316.9 1.6 pad_maximum_fusion.1.act_ref
  318.5 22.1 %all-gather.4.cloned.1.call-done.maps_ref = f32[2048,256]{1,0:T(8,128)} async-done(((f32[128,256]{1,0:T(8,128)}), f32[2048,256]{1,0:T(8,128)}) %all-gather.4.cloned.1.call-update) | async-done | bytes 2097168 | tf_op jit(solution)/shard_map/all_gather | solution.py:428
  340.6 18.0 %states.1 = (f32[8,64,512]{2,1,0:T(8,128)}, f32[2048,128]{1,0:T(8,128)}, f32[72,512]{1,0:T(8,128)}) custom-call(s32[1]{0:T(128)} %bitcast.refs_0_.place_ref, f32[2048,256]{1,0:T(8,128)} %all-gather.4.cloned.1.call-done.maps_ref, bf16[4,512,512]{2,1,0:T(8,128)(2,1)} %pad_maximum_fusion.1.act_ref, f32[128,128]{1,0:T(8,128)} %fusion.11.choice_ref, ...), custom_call_target="tpu_custom_call" | custom-call | tf_op jit(solution)/shard_map/states/pallas_call | solution.py:305
  358.6 1.3 collective-permute-start.17
  361.3 4.1 collective-permute-start.18
  365.4 4.2 collective-permute-start.19
  369.6 2.5 collective-permute-start.20
  372.1 1.3 collective-permute-start.21
  375.4 19.4 %inside.1.inside_ref = f32[2048,512]{1,0:T(8,128)} custom-call(s32[1]{0:T(128)} %bitcast.refs_0_.place_ref, f32[2048,256]{1,0:T(8,128)} %all-gather.4.cloned.1.call-done.maps_ref, bf16[4,512,512]{2,1,0:T(8,128)(2,1)} %pad_maximum_fusion.1.act_ref, f32[128,128]{1,0:T(8,128)} %fusion.11.choice_ref, f32[8,128]{1,0:T(8,128)} %fusion.17.choice_t_ref, ...), custom_call_target="tpu_custom_call" | custom-call | tf_op jit(solution)/shard_map/inside/pallas_call | solution.py:324
  394.8 1.3 collective-permute-start.23
  396.2 2.6 collective-permute-done.23
  399.6 10.0 %finish.1 = bf16[2048,512]{1,0:T(8,128)(2,1)} custom-call(f32[2048,512]{1,0:T(8,128)} %inside.1.inside_ref, f32[2048,256]{1,0:T(8,128)} %all-gather.4.cloned.1.call-done.maps_ref, f32[2048,128]{1,0:T(8,128)} %get-tuple-element.29.run_ref, f32[128,512]{1,0:T(8,128)} %fusion.1.spread_ref, f32[64,512]{1,0:T(8,128)} %fusion.2.entering_ref), custom_call_target="tpu_custom_call" | custom-call | tf_op jit(solution)/shard_map/finish/pallas_call | solution.py:352
  (88 shorter events, 16.3 us)
Async XLA Ops:
  6.5 191.6 %all-gather.6.cloned.1.call-start = ((), (), s32[]{:S(2)}) async-start(), calls=%async_computation.2 | async-start | bytes 34603008 | tf_op jit(solution)/shard_map/all_gather | solution.py:388
  8.8 7.4 %copy-start.9 = (s32[128,2]{0,1:T(2,128)S(1)}, s32[128,2]{0,1:T(2,128)}, u32[]{:S(2)}) copy-start(s32[128,2]{0,1:T(2,128)} %param.17) | copy-start | bytes 3076
  8.8 7.4 %copy-start.10 = (s32[128,2]{0,1:T(2,128)S(1)}, s32[128,2]{0,1:T(2,128)}, u32[]{:S(2)}) copy-start(s32[128,2]{0,1:T(2,128)} %param.16) | copy-start | bytes 3076
  8.8 8.2 %copy-start.8 = (f32[128,2]{0,1:T(2,128)S(1)}, f32[128,2]{0,1:T(2,128)}, u32[]{:S(2)}) copy-start(f32[128,2]{0,1:T(2,128)} %param.18) | copy-start | bytes 3076
  8.9 132.2 %all-to-all-start = ((bf16[1,1,16,24,8192]{4,3,1,0,2:T(8,128)(2,1)}), bf16[1,1,16,24,8192]{4,3,1,0,2:T(8,128)(2,1)}, u32[]{:S(2)}, u32[]{:S(2)}) async-start(bf16[1,1,16,24,8192]{4,3,1,0,2:T(8,128)(2,1)} %bitcast.65), calls=%async_computation | async-start | bytes 12582912 | tf_op jit(solution)/shard_map/all_to_all | solution.py:390
  16.2 324.5 %all-gather.4.cloned.1.call-start = ((), (), s32[]{:S(2)}) async-start(), calls=%async_computation.1 | async-start | bytes 2228224 | tf_op jit(solution)/shard_map/all_gather | solution.py:428
  141.0 13.2 %copy-start.3 = (bf16[512,128]{1,0:T(8,128)(2,1)S(1)}, bf16[512,128]{1,0:T(8,128)(2,1)}, u32[]{:S(2)}) copy-start(bf16[512,128]{1,0:T(8,128)(2,1)} %param.24) | copy-start | bytes 393220
  141.0 13.2 %copy-start.4 = (bf16[512,128]{1,0:T(8,128)(2,1)S(1)}, bf16[512,128]{1,0:T(8,128)(2,1)}, u32[]{:S(2)}) copy-start(bf16[512,128]{1,0:T(8,128)(2,1)} %param.23) | copy-start | bytes 393220
  141.0 13.3 %copy-start.6 = (f32[4,512]{1,0:T(4,128)S(1)}, f32[4,512]{1,0:T(4,128)}, u32[]{:S(2)}) copy-start(f32[4,512]{1,0:T(4,128)} %param.21) | copy-start | bytes 24580
  141.0 13.3 %copy-start.7 = (f32[512]{0:T(512)S(1)}, f32[512]{0:T(512)}, u32[]{:S(2)}) copy-start(f32[512]{0:T(512)} %param.22) | copy-start | bytes 6148
  150.9 45.8 %collective-permute-start = (bf16[128,8192]{1,0:T(8,128)(2,1)}, bf16[128,8192]{1,0:T(8,128)(2,1)S(1)}, u32[]{:S(2)}, u32[]{:S(2)}) collective-permute-start(bf16[128,8192]{1,0:T(8,128)(2,1)} %combine.1.refs_1_), channel_id=1, source_target_pairs={{0,1},{1,2},{2,3},{3,0},{4,5},{5,6},{6,7},{7,4},{8,9},{9,10},{10,1... | collective-permute-start | bytes 6291464 | tf_op jit(solution)/shard_map/ppermute | solution.py:23
  151.1 46.2 %collective-permute-start.2 = (bf16[128,8192]{1,0:T(8,128)(2,1)}, bf16[128,8192]{1,0:T(8,128)(2,1)}, u32[]{:S(2)}, u32[]{:S(2)}) collective-permute-start(bf16[128,8192]{1,0:T(8,128)(2,1)} %combine.1.refs_1_), channel_id=1, source_target_pairs={{0,3},{1,0},{2,1},{3,2},{4,7},{5,4},{6,5},{7,6},{8,11},{9,8},{10,9... | collective-permute-start | bytes 6291464 | tf_op jit(solution)/shard_map/ppermute | solution.py:23
  154.4 6.6 %collective-permute-start.6 = (f32[8,512]{1,0:T(8,128)S(1)}, f32[8,512]{1,0:T(8,128)S(1)}, u32[]{:S(2)}, u32[]{:S(2)}) collective-permute-start(f32[8,512]{1,0:T(8,128)S(1)} %maximum_maximum_fusion), channel_id=1, source_target_pairs={{0,12},{4,0},{8,4},{12,8},{1,13},{5,1},{9,5},{13,9},{2,14},{6,2},{... | collective-permute-start | bytes 49160 | tf_op jit(solution)/shard_map/ppermute | solution.py:23
  157.8 5.7 %collective-permute-start.7 = (f32[8,512]{1,0:T(8,128)S(1)}, f32[8,512]{1,0:T(8,128)S(1)}, u32[]{:S(2)}, u32[]{:S(2)}) collective-permute-start(f32[8,512]{1,0:T(8,128)S(1)} %maximum_maximum_fusion), channel_id=1, source_target_pairs={{0,8},{4,12},{8,0},{12,4},{1,9},{5,13},{9,1},{13,5},{2,10},{6,14},... | collective-permute-start | bytes 49160 | tf_op jit(solution)/shard_map/ppermute | solution.py:23
  159.6 6.2 %collective-permute-start.8 = (f32[8,512]{1,0:T(8,128)S(1)}, f32[8,512]{1,0:T(8,128)S(1)}, u32[]{:S(2)}, u32[]{:S(2)}) collective-permute-start(f32[8,512]{1,0:T(8,128)S(1)} %maximum_maximum_fusion), channel_id=1, source_target_pairs={{0,4},{4,8},{8,12},{12,0},{1,5},{5,9},{9,13},{13,1},{2,6},{6,10},{... | collective-permute-start | bytes 49160 | tf_op jit(solution)/shard_map/ppermute | solution.py:23
  160.9 15.8 %collective-permute-start.5 = (bf16[512,256]{1,0:T(8,128)(2,1)S(1)}, bf16[512,256]{1,0:T(8,128)(2,1)S(1)}, u32[]{:S(2)}, u32[]{:S(2)}) collective-permute-start(bf16[512,256]{1,0:T(8,128)(2,1)S(1)} %pad_maximum_fusion.5), channel_id=1, source_target_pairs={{0,4},{4,8},{8,12},{12,0},{1,5},{5,9},{9,13},{13,1},{2,6},{6,10},{... | collective-permute-start | bytes 786440 | tf_op jit(solution)/shard_map/ppermute | solution.py:23
  163.5 14.8 %collective-permute-start.3 = (bf16[512,256]{1,0:T(8,128)(2,1)S(1)}, bf16[512,256]{1,0:T(8,128)(2,1)S(1)}, u32[]{:S(2)}, u32[]{:S(2)}) collective-permute-start(bf16[512,256]{1,0:T(8,128)(2,1)S(1)} %pad_maximum_fusion.5), channel_id=1, source_target_pairs={{0,12},{4,0},{8,4},{12,8},{1,13},{5,1},{9,5},{13,9},{2,14},{6,2},{... | collective-permute-start | bytes 786440 | tf_op jit(solution)/shard_map/ppermute | solution.py:23
  165.8 20.6 %collective-permute-start.4 = (bf16[512,256]{1,0:T(8,128)(2,1)S(1)}, bf16[512,256]{1,0:T(8,128)(2,1)S(1)}, u32[]{:S(2)}, u32[]{:S(2)}) collective-permute-start(bf16[512,256]{1,0:T(8,128)(2,1)S(1)} %pad_maximum_fusion.5), channel_id=1, source_target_pairs={{0,8},{4,12},{8,0},{12,4},{1,9},{5,13},{9,1},{13,5},{2,10},{6,14},... | collective-permute-start | bytes 786440 | tf_op jit(solution)/shard_map/ppermute | solution.py:23
  196.7 3.7 copy-start
  196.8 36.7 %collective-permute-start.1 = (bf16[64,8192]{1,0:T(8,128)(2,1)S(1)}, bf16[64,8192]{1,0:T(8,128)(2,1)}, u32[]{:S(2)}, u32[]{:S(2)}) collective-permute-start(bf16[64,8192]{1,0:T(8,128)(2,1)S(1)} %slice.110), channel_id=1, source_target_pairs={{0,1},{1,2},{2,3},{3,0},{4,5},{5,6},{6,7},{7,4},{8,9},{9,10},{10,1... | collective-permute-start | bytes 3145736 | tf_op jit(solution)/shard_map/ppermute | solution.py:23
  200.4 33.0 %collective-permute-start.9 = (bf16[64,8192]{1,0:T(8,128)(2,1)}, bf16[64,8192]{1,0:T(8,128)(2,1)}, u32[]{:S(2)}, u32[]{:S(2)}) collective-permute-start(bf16[64,8192]{1,0:T(8,128)(2,1)} %slice.84), channel_id=1, source_target_pairs={{0,3},{1,0},{2,1},{3,2},{4,7},{5,4},{6,5},{7,6},{8,11},{9,8},{10,9... | collective-permute-start | bytes 3145736 | tf_op jit(solution)/shard_map/ppermute | solution.py:23
  211.5 20.5 %copy-start.2 = (bf16[1,3,128,512]{3,2,1,0:T(8,128)(2,1)S(1)}, bf16[1,3,128,512]{3,2,1,0:T(8,128)(2,1)}, u32[]{:S(2)}) copy-start(bf16[1,3,128,512]{3,2,1,0:T(8,128)(2,1)} %project.4) | copy-start | bytes 1179652
  251.9 6.3 %copy-start.1 = (bf16[3,1,128,512]{3,2,1,0:T(8,128)(2,1)S(1)}, bf16[3,1,128,512]{3,2,1,0:T(8,128)(2,1)}, u32[]{:S(2)}) copy-start(bf16[3,1,128,512]{3,2,1,0:T(8,128)(2,1)} %project.7) | copy-start | bytes 1179652
  259.0 7.6 %collective-permute-start.10 = (bf16[4,8,512]{2,1,0:T(8,128)(2,1)S(1)}, bf16[4,8,512]{2,1,0:T(8,128)(2,1)S(1)}, u32[]{:S(2)}, u32[]{:S(2)}) collective-permute-start(bf16[4,8,512]{2,1,0:T(8,128)(2,1)S(1)} %pad_maximum_fusion.7), channel_id=1, source_target_pairs={{0,4},{4,8},{8,12},{12,16},{16,20},{20,24},{24,28},{28,32},{32,36}... | collective-permute-start | bytes 98312 | tf_op jit(solution)/shard_map/ppermute | solution.py:28
  266.5 0.6 copy-start.5
  267.1 19.6 %copy-start.12 = (f32[8]{0:T(128)S(1)}, f32[8]{0:T(128)}, u32[]{:S(2)}) copy-start(f32[8]{0:T(128)} %param.26) | copy-start | bytes 100
  267.1 19.6 %copy-start.13 = (f32[8]{0:T(128)S(1)}, f32[8]{0:T(128)}, u32[]{:S(2)}) copy-start(f32[8]{0:T(128)} %param.25) | copy-start | bytes 100
  275.1 9.5 %collective-permute-start.11 = (f32[128,256]{1,0:T(8,128)S(1)}, f32[128,256]{1,0:T(8,128)S(1)}, u32[]{:S(2)}, u32[]{:S(2)}) collective-permute-start(f32[128,256]{1,0:T(8,128)S(1)} %get-tuple-element.43), channel_id=1, source_target_pairs={{0,1},{1,2},{2,3},{3,0},{4,5},{5,6},{6,7},{7,4},{8,9},{9,10},{10,1... | collective-permute-start | bytes 393224 | tf_op jit(solution)/shard_map/ppermute | solution.py:23
  277.1 7.4 %collective-permute-start.12 = (f32[128,256]{1,0:T(8,128)S(1)}, f32[128,256]{1,0:T(8,128)S(1)}, u32[]{:S(2)}, u32[]{:S(2)}) collective-permute-start(f32[128,256]{1,0:T(8,128)S(1)} %get-tuple-element.45), channel_id=1, source_target_pairs={{0,2},{1,3},{2,0},{3,1},{4,6},{5,7},{6,4},{7,5},{8,10},{9,11},{10,... | collective-permute-start | bytes 393224 | tf_op jit(solution)/shard_map/ppermute | solution.py:23
  277.8 7.3 %collective-permute-start.13 = (f32[128,256]{1,0:T(8,128)S(1)}, f32[128,256]{1,0:T(8,128)S(1)}, u32[]{:S(2)}, u32[]{:S(2)}) collective-permute-start(f32[128,256]{1,0:T(8,128)S(1)} %get-tuple-element.44), channel_id=1, source_target_pairs={{0,3},{1,0},{2,1},{3,2},{4,7},{5,4},{6,5},{7,6},{8,11},{9,8},{10,9... | collective-permute-start | bytes 393224 | tf_op jit(solution)/shard_map/ppermute | solution.py:23
  289.0 17.4 %collective-permute-start.14 = (bf16[512,512]{1,0:T(8,128)(2,1)S(1)}, bf16[512,512]{1,0:T(8,128)(2,1)S(1)}, u32[]{:S(2)}, u32[]{:S(2)}) collective-permute-start(bf16[512,512]{1,0:T(8,128)(2,1)S(1)} %get-tuple-element.39), channel_id=1, source_target_pairs={{0,4},{4,8},{8,12},{12,0},{1,5},{5,9},{9,13},{13,1},{2,6},{6,10},{... | collective-permute-start | bytes 1572872 | tf_op jit(solution)/shard_map/ppermute | solution.py:23
  290.7 25.7 %collective-permute-start.15 = (bf16[512,512]{1,0:T(8,128)(2,1)S(1)}, bf16[512,512]{1,0:T(8,128)(2,1)S(1)}, u32[]{:S(2)}, u32[]{:S(2)}) collective-permute-start(bf16[512,512]{1,0:T(8,128)(2,1)S(1)} %get-tuple-element.38), channel_id=1, source_target_pairs={{0,8},{4,12},{8,0},{12,4},{1,9},{5,13},{9,1},{13,5},{2,10},{6,14},... | collective-permute-start | bytes 1572872 | tf_op jit(solution)/shard_map/ppermute | solution.py:23
  292.7 24.2 %collective-permute-start.16 = (bf16[512,512]{1,0:T(8,128)(2,1)S(1)}, bf16[512,512]{1,0:T(8,128)(2,1)S(1)}, u32[]{:S(2)}, u32[]{:S(2)}) collective-permute-start(bf16[512,512]{1,0:T(8,128)(2,1)S(1)} %get-tuple-element.37), channel_id=1, source_target_pairs={{0,12},{4,0},{8,4},{12,8},{1,13},{5,1},{9,5},{13,9},{2,14},{6,2},{... | collective-permute-start | bytes 1572872 | tf_op jit(solution)/shard_map/ppermute | solution.py:23
  318.5 42.1 %copy-start.11 = (f32[8]{0:T(128)S(1)}, f32[8]{0:T(128)}, u32[]{:S(2)}) copy-start(f32[8]{0:T(128)} %param.27) | copy-start | bytes 100
  358.6 14.8 %collective-permute-start.17 = (f32[72,512]{1,0:T(8,128)}, f32[72,512]{1,0:T(8,128)S(1)}, u32[]{:S(2)}, u32[]{:S(2)}) collective-permute-start(f32[72,512]{1,0:T(8,128)} %get-tuple-element.30), channel_id=1, source_target_pairs={{0,16},{16,32},{32,48},{48,64},{64,80},{80,96},{96,112},{1,17},{17... | collective-permute-start | bytes 442376 | tf_op jit(solution)/shard_map/ppermute | solution.py:28
  361.3 33.5 %collective-permute-start.18 = (f32[72,512]{1,0:T(8,128)}, f32[72,512]{1,0:T(8,128)S(1)}, u32[]{:S(2)}, u32[]{:S(2)}) collective-permute-start(f32[72,512]{1,0:T(8,128)} %get-tuple-element.30), channel_id=1, source_target_pairs={{0,32},{16,48},{32,64},{48,80},{64,96},{80,112},{1,33},{17,49},{33... | collective-permute-start | bytes 442376 | tf_op jit(solution)/shard_map/ppermute | solution.py:28
  365.4 30.7 %collective-permute-start.19 = (f32[72,512]{1,0:T(8,128)}, f32[72,512]{1,0:T(8,128)S(1)}, u32[]{:S(2)}, u32[]{:S(2)}) collective-permute-start(f32[72,512]{1,0:T(8,128)} %get-tuple-element.30), channel_id=1, source_target_pairs={{0,48},{16,64},{32,80},{48,96},{64,112},{1,49},{17,65},{33,81},{49... | collective-permute-start | bytes 442376 | tf_op jit(solution)/shard_map/ppermute | solution.py:28
  369.6 26.6 %collective-permute-start.20 = (f32[72,512]{1,0:T(8,128)}, f32[72,512]{1,0:T(8,128)S(1)}, u32[]{:S(2)}, u32[]{:S(2)}) collective-permute-start(f32[72,512]{1,0:T(8,128)} %get-tuple-element.30), channel_id=1, source_target_pairs={{0,64},{16,80},{32,96},{48,112},{1,65},{17,81},{33,97},{49,113},{2... | collective-permute-start | bytes 442376 | tf_op jit(solution)/shard_map/ppermute | solution.py:28
  372.1 24.1 %collective-permute-start.21 = (f32[72,512]{1,0:T(8,128)}, f32[72,512]{1,0:T(8,128)S(1)}, u32[]{:S(2)}, u32[]{:S(2)}) collective-permute-start(f32[72,512]{1,0:T(8,128)} %get-tuple-element.30), channel_id=1, source_target_pairs={{0,80},{16,96},{32,112},{1,81},{17,97},{33,113},{2,82},{18,98},{34... | collective-permute-start | bytes 442376 | tf_op jit(solution)/shard_map/ppermute | solution.py:28
  373.4 22.8 %collective-permute-start.22 = (f32[72,512]{1,0:T(8,128)}, f32[72,512]{1,0:T(8,128)S(1)}, u32[]{:S(2)}, u32[]{:S(2)}) collective-permute-start(f32[72,512]{1,0:T(8,128)} %get-tuple-element.30), channel_id=1, source_target_pairs={{0,96},{16,112},{1,97},{17,113},{2,98},{18,114},{3,99},{19,115},{4... | collective-permute-start | bytes 442376 | tf_op jit(solution)/shard_map/ppermute | solution.py:28
  375.4 19.4 %copy-start.14 = (f32[72,512]{1,0:T(8,128)S(1)}, f32[72,512]{1,0:T(8,128)}, u32[]{:S(2)}) copy-start(f32[72,512]{1,0:T(8,128)} %get-tuple-element.30) | copy-start | bytes 442372
  394.8 4.0 collective-permute-start.23
Sparse Core Ops, SparseCore 0:
  9.6 188.4 all-gather.5
  286.8 53.7 all-gather.3

commit v4 on v3

--- a/solution.py
+++ b/solution.py
@@ -401,7 +401,7 @@
     half = own // 2
     far = jnp.concatenate([shifted(below[:half], "y", 1), shifted(above[half:], "y", -1)], axis=0)
 
-    deep = 2
+    deep = 4
     own_spec = pl.BlockSpec((deep * depth, local), lambda r, k, _: (k, 0))
     other_spec = pl.BlockSpec((deep, 1, depth, local), lambda r, k, p: (k, (p[0] + r + 1) % nx, 0, 0))
     steps = spans // deep

time: 418 us -> 410 us (0.981)
  Pallas kernels: 115 us -> 107 us
    pallas_call x4, Pallas kernels: 51.3 us -> 43.2 us  [project(): pl.pallas_call(project_body, name='project', grid_spec=pltpu.PrefetchScal...]
  transfers between devices with their start and end apart: 27 -> 27, of which waited for: 14 -> 14; matrix products, arithmetic and copies ran while one was open for 4% -> 4% of each run, Pallas kernels for 14% -> 13%
where the time goes in v4:
time: 410 us; the launch traced here: 408 us
  waiting for transfers between devices  206 us (50%)
  Pallas kernels  107 us (26%)
  starting transfers between devices  53.7 us (13%)
  other arithmetic  14.9 us (4%)
  between operations  13.7 us (3%)
  local copies, waits for them, and re-layouts  12.9 us (3%)
    all_to_all x1, waiting for transfers between devices, shards(): lax.all_to_all(expert_rows, PLANE, split_axis=2, concat_axis=1, tiled=True)  123 us
    ppermute x16, waiting for transfers between devices, shifted(): lax.ppermute(value, axis, [(i, (i + steps) % count) for i in range(count)])  57 us
    pallas_call x4, Pallas kernels, project(): pl.pallas_call(project_body, name='project', grid_spec=pltpu.PrefetchScal...  43.2 us
    ppermute x16, starting transfers between devices, shifted(): lax.ppermute(value, axis, [(i, (i + steps) % count) for i in range(count)])  25.9 us
    all_gather x1, waiting for transfers between devices, shards(): maps = lax.all_gather(mine, PLANE, axis=0, tiled=True)  22.2 us
    ppermute x8, starting transfers between devices, passed_on(): lax.ppermute(value, axes, [(i, i + steps) for i in range(count - steps)])  20.4 us
    pallas_call x1, Pallas kernels, scan_output(): pl.pallas_call(inside_body, name='inside', grid_spec=pltpu.PrefetchScalar...  19.4 us
    pallas_call x1, Pallas kernels, scan_output(): pl.pallas_call(state_body, name='states', grid_spec=pltpu.PrefetchScalarG...  18 us
  transfers between devices with their start and end apart: 27, of which 14 were waited for; matrix products, arithmetic and copies ran while one was open for 4% of the time, Pallas kernels for 13%

profile of v4, /device:TPU:0, one launch (start us, length us, event | category | flops | bytes accessed | tf_op | source)
XLA Modules:
  0.0 408.4 jit_solution(14048616739082264070)
XLA Ops:
  6.5 2.3 constant_dynamic-slice_fusion
  8.9 7.3 %all-to-all-start = ((bf16[1,1,16,24,8192]{4,3,1,0,2:T(8,128)(2,1)}), bf16[1,1,16,24,8192]{4,3,1,0,2:T(8,128)(2,1)}, u32[]{:S(2)}, u32[]{:S(2)}) async-start(bf16[1,1,16,24,8192]{4,3,1,0,2:T(8,128)(2,1)} %bitcast.65), calls=%async_computation | async-start | bytes 12582912 | tf_op jit(solution)/shard_map/all_to_all | solution.py:390
  17.8 123.3 %all-to-all-done = bf16[1,1,16,24,8192]{4,3,1,0,2:T(8,128)(2,1)} async-done(((bf16[1,1,16,24,8192]{4,3,1,0,2:T(8,128)(2,1)}), bf16[1,1,16,24,8192]{4,3,1,0,2:T(8,128)(2,1)}, u32[]{:S(2)}, u32[]{:S(2)}) %all-to-all-start) | async-done | bytes 6291488 | tf_op jit(solution)/shard_map/all_to_all | solution.py:390
  141.0 9.9 %combine.1.refs_1_ = bf16[128,8192]{1,0:T(8,128)(2,1)} custom-call(s32[128,2]{1,0:T(8,128)} %copy.42.index_ref, f32[128,2]{1,0:T(8,128)} %copy.43.weight_ref, bf16[384,8192]{1,0:T(8,128)(2,1)} %bitcast.3.rows_ref, bf16[128,8192]{1,0:T(8,128)(2,1)} %residual_ref.1, f32[1,8192]{1,0:T(1,128)} %bitcast.81), custom_call_target="tpu_custom_call" | custom-call | tf_op jit(solution)/shard_map/combine/pallas_call | solution.py:70
  151.1 3.1 collective-permute-start.2
  154.4 3.4 collective-permute-start.6
  157.8 1.8 collective-permute-start.7
  159.6 1.3 collective-permute-start.8
  161.7 1.8 collective-permute-done.7
  163.5 2.3 collective-permute-start.3
  166.5 10.2 %collective-permute-done.5 = bf16[512,256]{1,0:T(8,128)(2,1)S(1)} collective-permute-done((bf16[512,256]{1,0:T(8,128)(2,1)S(1)}, bf16[512,256]{1,0:T(8,128)(2,1)S(1)}, u32[]{:S(2)}, u32[]{:S(2)}) %collective-permute-start.5) | collective-permute-done | bytes 262176 | tf_op jit(solution)/shard_map/ppermute | solution.py:23
  176.7 1.5 collective-permute-done.3
  178.2 8.2 %collective-permute-done.4 = bf16[512,256]{1,0:T(8,128)(2,1)S(1)} collective-permute-done((bf16[512,256]{1,0:T(8,128)(2,1)S(1)}, bf16[512,256]{1,0:T(8,128)(2,1)S(1)}, u32[]{:S(2)}, u32[]{:S(2)}) %collective-permute-start.4) | collective-permute-done | bytes 262176 | tf_op jit(solution)/shard_map/ppermute | solution.py:23
  187.5 9.1 %collective-permute-done.refs_3_ = bf16[128,8192]{1,0:T(8,128)(2,1)S(1)} collective-permute-done((bf16[128,8192]{1,0:T(8,128)(2,1)}, bf16[128,8192]{1,0:T(8,128)(2,1)S(1)}, u32[]{:S(2)}, u32[]{:S(2)}) %collective-permute-start) | collective-permute-done | bytes 2097184 | tf_op jit(solution)/shard_map/ppermute | solution.py:23
  198.1 2.3 slice.84
  200.4 2.0 collective-permute-start.9
  202.4 8.6 %project.4 = bf16[1,3,128,512]{3,2,1,0:T(8,128)(2,1)} custom-call(s32[1]{0:T(128)} %bitcast.refs_0_.place_ref, bf16[128,8192]{1,0:T(8,128)(2,1)} %combine.1.refs_1_, bf16[128,8192]{1,0:T(8,128)(2,1)} %collective-permute-done.2.refs_2_, bf16[128,8192]{1,0:T(8,128)(2,1)} %copy-done, bf16[8192,512]{1,0:T(8,128)(2,1)} %refs_2_.1), custom_call_target="tpu_custom_call" | custom-call | tf_op jit(solution)/shard_map/project/pallas_call | solution.py:105
  210.9 17.2 %project.5 = bf16[3,3,128,512]{3,2,1,0:T(8,128)(2,1)} custom-call(s32[1]{0:T(128)} %bitcast.refs_0_.place_ref, bf16[128,8192]{1,0:T(8,128)(2,1)} %combine.1.refs_1_, bf16[128,8192]{1,0:T(8,128)(2,1)} %collective-permute-done.2.refs_2_, bf16[128,8192]{1,0:T(8,128)(2,1)} %copy-done, bf16[8,4,1024,512]{3,2,1,0:T(8,128)(2,1)} %bitcast.63), custom_call_target="tpu_custom_call" | custom-call | tf_op jit(solution)/shard_map/project/pallas_call | solution.py:105
  228.1 1.4 pad_maximum_fusion.2
  229.6 3.0 pad_maximum_fusion.refs_1_
  232.6 12.0 %project.7 = bf16[3,1,128,512]{3,2,1,0:T(8,128)(2,1)} custom-call(s32[1]{0:T(128)} %bitcast.refs_0_.place_ref, bf16[128,8192]{1,0:T(8,128)(2,1)} %pad_maximum_fusion.refs_1_, bf16[8,4,1024,512]{3,2,1,0:T(8,128)(2,1)} %bitcast.64), custom_call_target="tpu_custom_call" | custom-call | tf_op jit(solution)/shard_map/project/pallas_call | solution.py:105
  244.6 5.5 %project.6 = bf16[1,1,128,512]{3,2,1,0:T(8,128)(2,1)} custom-call(s32[1]{0:T(128)} %bitcast.refs_0_.place_ref, bf16[128,8192]{1,0:T(8,128)(2,1)} %pad_maximum_fusion.refs_1_, bf16[8192,512]{1,0:T(8,128)(2,1)} %refs_2_.1), custom_call_target="tpu_custom_call" | custom-call | tf_op jit(solution)/shard_map/project/pallas_call | solution.py:105
  250.9 4.5 %collective-permute-start.10 = (bf16[4,8,512]{2,1,0:T(8,128)(2,1)S(1)}, bf16[4,8,512]{2,1,0:T(8,128)(2,1)S(1)}, u32[]{:S(2)}, u32[]{:S(2)}) collective-permute-start(bf16[4,8,512]{2,1,0:T(8,128)(2,1)S(1)} %pad_maximum_fusion.7), channel_id=1, source_target_pairs={{0,4},{4,8},{8,12},{12,16},{16,20},{20,24},{24,28},{28,32},{32,36}... | collective-permute-start | bytes 98312 | tf_op jit(solution)/shard_map/ppermute | solution.py:28
  255.4 1.7 fusion.far_ref
  257.2 1.4 copy.48.near_ref
  259.1 6.8 %filter.1 = (bf16[4,512,512]{2,1,0:T(8,128)(2,1)}, f32[512,256]{1,0:T(8,128)}) custom-call(s32[1]{0:T(128)} %bitcast.1.place_ref, bf16[4,3,128,512]{3,2,1,0:T(8,128)(2,1)} %copy.48.near_ref, bf16[4,1,128,512]{3,2,1,0:T(8,128)(2,1)} %fusion.far_ref, bf16[4,8,512]{2,1,0:T(8,128)(2,1)} %copy-done.5, f32[4,8,512]{2,1,0:T(8,128)} %pad_maximum_fusion.6.taps_ref, ...), custom_call_target="tpu_custom_call" | custom-call | tf_op jit(solution)/shard_map/filter/pallas_call | solution.py:154
  267.0 2.1 collective-permute-start.11
  269.8 2.5 collective-permute-start.13
  272.3 4.2 %collective-permute-done.11 = f32[128,256]{1,0:T(8,128)S(1)} collective-permute-done((f32[128,256]{1,0:T(8,128)S(1)}, f32[128,256]{1,0:T(8,128)S(1)}, u32[]{:S(2)}, u32[]{:S(2)}) %collective-permute-start.11) | collective-permute-done | bytes 131104 | tf_op jit(solution)/shard_map/ppermute | solution.py:23
  277.1 1.6 fusion.9
  279.4 1.7 fusion.21
  281.0 1.7 collective-permute-start.14
  282.7 2.0 collective-permute-start.15
  284.7 1.4 collective-permute-start.16
  287.6 10.8 %collective-permute-done.14 = bf16[512,512]{1,0:T(8,128)(2,1)S(1)} collective-permute-done((bf16[512,512]{1,0:T(8,128)(2,1)S(1)}, bf16[512,512]{1,0:T(8,128)(2,1)S(1)}, u32[]{:S(2)}, u32[]{:S(2)}) %collective-permute-start.14) | collective-permute-done | bytes 524320 | tf_op jit(solution)/shard_map/ppermute | solution.py:23
  298.3 10.1 %collective-permute-done.15 = bf16[512,512]{1,0:T(8,128)(2,1)S(1)} collective-permute-done((bf16[512,512]{1,0:T(8,128)(2,1)S(1)}, bf16[512,512]{1,0:T(8,128)(2,1)S(1)}, u32[]{:S(2)}, u32[]{:S(2)}) %collective-permute-start.15) | collective-permute-done | bytes 524320 | tf_op jit(solution)/shard_map/ppermute | solution.py:23
  308.9 1.6 pad_maximum_fusion.1.act_ref
  310.5 22.2 %all-gather.4.cloned.1.call-done.maps_ref = f32[2048,256]{1,0:T(8,128)} async-done(((f32[128,256]{1,0:T(8,128)}), f32[2048,256]{1,0:T(8,128)}) %all-gather.4.cloned.1.call-update) | async-done | bytes 2097168 | tf_op jit(solution)/shard_map/all_gather | solution.py:428
  332.6 18.0 %states.1 = (f32[8,64,512]{2,1,0:T(8,128)}, f32[2048,128]{1,0:T(8,128)}, f32[72,512]{1,0:T(8,128)}) custom-call(s32[1]{0:T(128)} %bitcast.refs_0_.place_ref, f32[2048,256]{1,0:T(8,128)} %all-gather.4.cloned.1.call-done.maps_ref, bf16[4,512,512]{2,1,0:T(8,128)(2,1)} %pad_maximum_fusion.1.act_ref, f32[128,128]{1,0:T(8,128)} %fusion.11.choice_ref, ...), custom_call_target="tpu_custom_call" | custom-call | tf_op jit(solution)/shard_map/states/pallas_call | solution.py:305
  350.6 1.3 collective-permute-start.17
  353.3 4.1 collective-permute-start.18
  357.4 4.1 %collective-permute-start.19 = (f32[72,512]{1,0:T(8,128)}, f32[72,512]{1,0:T(8,128)S(1)}, u32[]{:S(2)}, u32[]{:S(2)}) collective-permute-start(f32[72,512]{1,0:T(8,128)} %get-tuple-element.30), channel_id=1, source_target_pairs={{0,48},{16,64},{32,80},{48,96},{64,112},{1,49},{17,65},{33,81},{49... | collective-permute-start | bytes 442376 | tf_op jit(solution)/shard_map/ppermute | solution.py:28
  361.6 2.5 collective-permute-start.20
  364.1 1.3 collective-permute-start.21
  367.4 19.4 %inside.1.inside_ref = f32[2048,512]{1,0:T(8,128)} custom-call(s32[1]{0:T(128)} %bitcast.refs_0_.place_ref, f32[2048,256]{1,0:T(8,128)} %all-gather.4.cloned.1.call-done.maps_ref, bf16[4,512,512]{2,1,0:T(8,128)(2,1)} %pad_maximum_fusion.1.act_ref, f32[128,128]{1,0:T(8,128)} %fusion.11.choice_ref, f32[8,128]{1,0:T(8,128)} %fusion.17.choice_t_ref, ...), custom_call_target="tpu_custom_call" | custom-call | tf_op jit(solution)/shard_map/inside/pallas_call | solution.py:324
  386.8 1.3 collective-permute-start.23
  388.2 2.6 collective-permute-done.23
  391.6 10.0 %finish.1 = bf16[2048,512]{1,0:T(8,128)(2,1)} custom-call(f32[2048,512]{1,0:T(8,128)} %inside.1.inside_ref, f32[2048,256]{1,0:T(8,128)} %all-gather.4.cloned.1.call-done.maps_ref, f32[2048,128]{1,0:T(8,128)} %get-tuple-element.29.run_ref, f32[128,512]{1,0:T(8,128)} %fusion.1.spread_ref, f32[64,512]{1,0:T(8,128)} %fusion.2.entering_ref), custom_call_target="tpu_custom_call" | custom-call | tf_op jit(solution)/shard_map/finish/pallas_call | solution.py:352
  (88 shorter events, 16.2 us)
Async XLA Ops:
  6.5 191.6 %all-gather.6.cloned.1.call-start = ((), (), s32[]{:S(2)}) async-start(), calls=%async_computation.2 | async-start | bytes 34603008 | tf_op jit(solution)/shard_map/all_gather | solution.py:388
  8.8 7.4 %copy-start.9 = (s32[128,2]{0,1:T(2,128)S(1)}, s32[128,2]{0,1:T(2,128)}, u32[]{:S(2)}) copy-start(s32[128,2]{0,1:T(2,128)} %param.17) | copy-start | bytes 3076
  8.8 7.4 %copy-start.10 = (s32[128,2]{0,1:T(2,128)S(1)}, s32[128,2]{0,1:T(2,128)}, u32[]{:S(2)}) copy-start(s32[128,2]{0,1:T(2,128)} %param.16) | copy-start | bytes 3076
  8.8 8.2 %copy-start.8 = (f32[128,2]{0,1:T(2,128)S(1)}, f32[128,2]{0,1:T(2,128)}, u32[]{:S(2)}) copy-start(f32[128,2]{0,1:T(2,128)} %param.18) | copy-start | bytes 3076
  8.9 132.2 %all-to-all-start = ((bf16[1,1,16,24,8192]{4,3,1,0,2:T(8,128)(2,1)}), bf16[1,1,16,24,8192]{4,3,1,0,2:T(8,128)(2,1)}, u32[]{:S(2)}, u32[]{:S(2)}) async-start(bf16[1,1,16,24,8192]{4,3,1,0,2:T(8,128)(2,1)} %bitcast.65), calls=%async_computation | async-start | bytes 12582912 | tf_op jit(solution)/shard_map/all_to_all | solution.py:390
  16.2 316.5 %all-gather.4.cloned.1.call-start = ((), (), s32[]{:S(2)}) async-start(), calls=%async_computation.1 | async-start | bytes 2228224 | tf_op jit(solution)/shard_map/all_gather | solution.py:428
  141.0 13.2 %copy-start.3 = (bf16[512,128]{1,0:T(8,128)(2,1)S(1)}, bf16[512,128]{1,0:T(8,128)(2,1)}, u32[]{:S(2)}) copy-start(bf16[512,128]{1,0:T(8,128)(2,1)} %param.24) | copy-start | bytes 393220
  141.0 13.2 %copy-start.4 = (bf16[512,128]{1,0:T(8,128)(2,1)S(1)}, bf16[512,128]{1,0:T(8,128)(2,1)}, u32[]{:S(2)}) copy-start(bf16[512,128]{1,0:T(8,128)(2,1)} %param.23) | copy-start | bytes 393220
  141.0 13.3 %copy-start.6 = (f32[4,512]{1,0:T(4,128)S(1)}, f32[4,512]{1,0:T(4,128)}, u32[]{:S(2)}) copy-start(f32[4,512]{1,0:T(4,128)} %param.21) | copy-start | bytes 24580
  141.0 13.3 %copy-start.7 = (f32[512]{0:T(512)S(1)}, f32[512]{0:T(512)}, u32[]{:S(2)}) copy-start(f32[512]{0:T(512)} %param.22) | copy-start | bytes 6148
  150.9 45.8 %collective-permute-start = (bf16[128,8192]{1,0:T(8,128)(2,1)}, bf16[128,8192]{1,0:T(8,128)(2,1)S(1)}, u32[]{:S(2)}, u32[]{:S(2)}) collective-permute-start(bf16[128,8192]{1,0:T(8,128)(2,1)} %combine.1.refs_1_), channel_id=1, source_target_pairs={{0,1},{1,2},{2,3},{3,0},{4,5},{5,6},{6,7},{7,4},{8,9},{9,10},{10,1... | collective-permute-start | bytes 6291464 | tf_op jit(solution)/shard_map/ppermute | solution.py:23
  151.1 46.2 %collective-permute-start.2 = (bf16[128,8192]{1,0:T(8,128)(2,1)}, bf16[128,8192]{1,0:T(8,128)(2,1)}, u32[]{:S(2)}, u32[]{:S(2)}) collective-permute-start(bf16[128,8192]{1,0:T(8,128)(2,1)} %combine.1.refs_1_), channel_id=1, source_target_pairs={{0,3},{1,0},{2,1},{3,2},{4,7},{5,4},{6,5},{7,6},{8,11},{9,8},{10,9... | collective-permute-start | bytes 6291464 | tf_op jit(solution)/shard_map/ppermute | solution.py:23
  154.4 6.6 %collective-permute-start.6 = (f32[8,512]{1,0:T(8,128)S(1)}, f32[8,512]{1,0:T(8,128)S(1)}, u32[]{:S(2)}, u32[]{:S(2)}) collective-permute-start(f32[8,512]{1,0:T(8,128)S(1)} %maximum_maximum_fusion), channel_id=1, source_target_pairs={{0,12},{4,0},{8,4},{12,8},{1,13},{5,1},{9,5},{13,9},{2,14},{6,2},{... | collective-permute-start | bytes 49160 | tf_op jit(solution)/shard_map/ppermute | solution.py:23
  157.8 5.7 %collective-permute-start.7 = (f32[8,512]{1,0:T(8,128)S(1)}, f32[8,512]{1,0:T(8,128)S(1)}, u32[]{:S(2)}, u32[]{:S(2)}) collective-permute-start(f32[8,512]{1,0:T(8,128)S(1)} %maximum_maximum_fusion), channel_id=1, source_target_pairs={{0,8},{4,12},{8,0},{12,4},{1,9},{5,13},{9,1},{13,5},{2,10},{6,14},... | collective-permute-start | bytes 49160 | tf_op jit(solution)/shard_map/ppermute | solution.py:23
  159.6 6.2 %collective-permute-start.8 = (f32[8,512]{1,0:T(8,128)S(1)}, f32[8,512]{1,0:T(8,128)S(1)}, u32[]{:S(2)}, u32[]{:S(2)}) collective-permute-start(f32[8,512]{1,0:T(8,128)S(1)} %maximum_maximum_fusion), channel_id=1, source_target_pairs={{0,4},{4,8},{8,12},{12,0},{1,5},{5,9},{9,13},{13,1},{2,6},{6,10},{... | collective-permute-start | bytes 49160 | tf_op jit(solution)/shard_map/ppermute | solution.py:23
  160.9 15.8 %collective-permute-start.5 = (bf16[512,256]{1,0:T(8,128)(2,1)S(1)}, bf16[512,256]{1,0:T(8,128)(2,1)S(1)}, u32[]{:S(2)}, u32[]{:S(2)}) collective-permute-start(bf16[512,256]{1,0:T(8,128)(2,1)S(1)} %pad_maximum_fusion.5), channel_id=1, source_target_pairs={{0,4},{4,8},{8,12},{12,0},{1,5},{5,9},{9,13},{13,1},{2,6},{6,10},{... | collective-permute-start | bytes 786440 | tf_op jit(solution)/shard_map/ppermute | solution.py:23
  163.5 14.8 %collective-permute-start.3 = (bf16[512,256]{1,0:T(8,128)(2,1)S(1)}, bf16[512,256]{1,0:T(8,128)(2,1)S(1)}, u32[]{:S(2)}, u32[]{:S(2)}) collective-permute-start(bf16[512,256]{1,0:T(8,128)(2,1)S(1)} %pad_maximum_fusion.5), channel_id=1, source_target_pairs={{0,12},{4,0},{8,4},{12,8},{1,13},{5,1},{9,5},{13,9},{2,14},{6,2},{... | collective-permute-start | bytes 786440 | tf_op jit(solution)/shard_map/ppermute | solution.py:23
  165.8 20.6 %collective-permute-start.4 = (bf16[512,256]{1,0:T(8,128)(2,1)S(1)}, bf16[512,256]{1,0:T(8,128)(2,1)S(1)}, u32[]{:S(2)}, u32[]{:S(2)}) collective-permute-start(bf16[512,256]{1,0:T(8,128)(2,1)S(1)} %pad_maximum_fusion.5), channel_id=1, source_target_pairs={{0,8},{4,12},{8,0},{12,4},{1,9},{5,13},{9,1},{13,5},{2,10},{6,14},... | collective-permute-start | bytes 786440 | tf_op jit(solution)/shard_map/ppermute | solution.py:23
  196.7 3.7 copy-start
  196.8 32.8 %collective-permute-start.1 = (bf16[64,8192]{1,0:T(8,128)(2,1)S(1)}, bf16[64,8192]{1,0:T(8,128)(2,1)}, u32[]{:S(2)}, u32[]{:S(2)}) collective-permute-start(bf16[64,8192]{1,0:T(8,128)(2,1)S(1)} %slice.110), channel_id=1, source_target_pairs={{0,1},{1,2},{2,3},{3,0},{4,5},{5,6},{6,7},{7,4},{8,9},{9,10},{10,1... | collective-permute-start | bytes 3145736 | tf_op jit(solution)/shard_map/ppermute | solution.py:23
  200.4 29.2 %collective-permute-start.9 = (bf16[64,8192]{1,0:T(8,128)(2,1)}, bf16[64,8192]{1,0:T(8,128)(2,1)}, u32[]{:S(2)}, u32[]{:S(2)}) collective-permute-start(bf16[64,8192]{1,0:T(8,128)(2,1)} %slice.84), channel_id=1, source_target_pairs={{0,3},{1,0},{2,1},{3,2},{4,7},{5,4},{6,5},{7,6},{8,11},{9,8},{10,9... | collective-permute-start | bytes 3145736 | tf_op jit(solution)/shard_map/ppermute | solution.py:23
  210.9 17.2 %copy-start.2 = (bf16[1,3,128,512]{3,2,1,0:T(8,128)(2,1)S(1)}, bf16[1,3,128,512]{3,2,1,0:T(8,128)(2,1)}, u32[]{:S(2)}) copy-start(bf16[1,3,128,512]{3,2,1,0:T(8,128)(2,1)} %project.4) | copy-start | bytes 1179652
  244.6 5.5 %copy-start.1 = (bf16[3,1,128,512]{3,2,1,0:T(8,128)(2,1)S(1)}, bf16[3,1,128,512]{3,2,1,0:T(8,128)(2,1)}, u32[]{:S(2)}) copy-start(bf16[3,1,128,512]{3,2,1,0:T(8,128)(2,1)} %project.7) | copy-start | bytes 1179652
  250.9 7.6 %collective-permute-start.10 = (bf16[4,8,512]{2,1,0:T(8,128)(2,1)S(1)}, bf16[4,8,512]{2,1,0:T(8,128)(2,1)S(1)}, u32[]{:S(2)}, u32[]{:S(2)}) collective-permute-start(bf16[4,8,512]{2,1,0:T(8,128)(2,1)S(1)} %pad_maximum_fusion.7), channel_id=1, source_target_pairs={{0,4},{4,8},{8,12},{12,16},{16,20},{20,24},{24,28},{28,32},{32,36}... | collective-permute-start | bytes 98312 | tf_op jit(solution)/shard_map/ppermute | solution.py:28
  258.5 0.6 copy-start.5
  259.1 19.6 %copy-start.12 = (f32[8]{0:T(128)S(1)}, f32[8]{0:T(128)}, u32[]{:S(2)}) copy-start(f32[8]{0:T(128)} %param.26) | copy-start | bytes 100
  259.1 19.6 %copy-start.13 = (f32[8]{0:T(128)S(1)}, f32[8]{0:T(128)}, u32[]{:S(2)}) copy-start(f32[8]{0:T(128)} %param.25) | copy-start | bytes 100
  267.0 9.5 %collective-permute-start.11 = (f32[128,256]{1,0:T(8,128)S(1)}, f32[128,256]{1,0:T(8,128)S(1)}, u32[]{:S(2)}, u32[]{:S(2)}) collective-permute-start(f32[128,256]{1,0:T(8,128)S(1)} %get-tuple-element.43), channel_id=1, source_target_pairs={{0,1},{1,2},{2,3},{3,0},{4,5},{5,6},{6,7},{7,4},{8,9},{9,10},{10,1... | collective-permute-start | bytes 393224 | tf_op jit(solution)/shard_map/ppermute | solution.py:23
  269.1 7.4 %collective-permute-start.12 = (f32[128,256]{1,0:T(8,128)S(1)}, f32[128,256]{1,0:T(8,128)S(1)}, u32[]{:S(2)}, u32[]{:S(2)}) collective-permute-start(f32[128,256]{1,0:T(8,128)S(1)} %get-tuple-element.45), channel_id=1, source_target_pairs={{0,2},{1,3},{2,0},{3,1},{4,6},{5,7},{6,4},{7,5},{8,10},{9,11},{10,... | collective-permute-start | bytes 393224 | tf_op jit(solution)/shard_map/ppermute | solution.py:23
  269.8 7.3 %collective-permute-start.13 = (f32[128,256]{1,0:T(8,128)S(1)}, f32[128,256]{1,0:T(8,128)S(1)}, u32[]{:S(2)}, u32[]{:S(2)}) collective-permute-start(f32[128,256]{1,0:T(8,128)S(1)} %get-tuple-element.44), channel_id=1, source_target_pairs={{0,3},{1,0},{2,1},{3,2},{4,7},{5,4},{6,5},{7,6},{8,11},{9,8},{10,9... | collective-permute-start | bytes 393224 | tf_op jit(solution)/shard_map/ppermute | solution.py:23
  281.0 17.3 %collective-permute-start.14 = (bf16[512,512]{1,0:T(8,128)(2,1)S(1)}, bf16[512,512]{1,0:T(8,128)(2,1)S(1)}, u32[]{:S(2)}, u32[]{:S(2)}) collective-permute-start(bf16[512,512]{1,0:T(8,128)(2,1)S(1)} %get-tuple-element.39), channel_id=1, source_target_pairs={{0,4},{4,8},{8,12},{12,0},{1,5},{5,9},{9,13},{13,1},{2,6},{6,10},{... | collective-permute-start | bytes 1572872 | tf_op jit(solution)/shard_map/ppermute | solution.py:23
  282.7 25.7 %collective-permute-start.15 = (bf16[512,512]{1,0:T(8,128)(2,1)S(1)}, bf16[512,512]{1,0:T(8,128)(2,1)S(1)}, u32[]{:S(2)}, u32[]{:S(2)}) collective-permute-start(bf16[512,512]{1,0:T(8,128)(2,1)S(1)} %get-tuple-element.38), channel_id=1, source_target_pairs={{0,8},{4,12},{8,0},{12,4},{1,9},{5,13},{9,1},{13,5},{2,10},{6,14},... | collective-permute-start | bytes 1572872 | tf_op jit(solution)/shard_map/ppermute | solution.py:23
  284.7 24.2 %collective-permute-start.16 = (bf16[512,512]{1,0:T(8,128)(2,1)S(1)}, bf16[512,512]{1,0:T(8,128)(2,1)S(1)}, u32[]{:S(2)}, u32[]{:S(2)}) collective-permute-start(bf16[512,512]{1,0:T(8,128)(2,1)S(1)} %get-tuple-element.37), channel_id=1, source_target_pairs={{0,12},{4,0},{8,4},{12,8},{1,13},{5,1},{9,5},{13,9},{2,14},{6,2},{... | collective-permute-start | bytes 1572872 | tf_op jit(solution)/shard_map/ppermute | solution.py:23
  310.5 42.1 %copy-start.11 = (f32[8]{0:T(128)S(1)}, f32[8]{0:T(128)}, u32[]{:S(2)}) copy-start(f32[8]{0:T(128)} %param.27) | copy-start | bytes 100
  350.6 14.8 %collective-permute-start.17 = (f32[72,512]{1,0:T(8,128)}, f32[72,512]{1,0:T(8,128)S(1)}, u32[]{:S(2)}, u32[]{:S(2)}) collective-permute-start(f32[72,512]{1,0:T(8,128)} %get-tuple-element.30), channel_id=1, source_target_pairs={{0,16},{16,32},{32,48},{48,64},{64,80},{80,96},{96,112},{1,17},{17... | collective-permute-start | bytes 442376 | tf_op jit(solution)/shard_map/ppermute | solution.py:28
  353.3 33.5 %collective-permute-start.18 = (f32[72,512]{1,0:T(8,128)}, f32[72,512]{1,0:T(8,128)S(1)}, u32[]{:S(2)}, u32[]{:S(2)}) collective-permute-start(f32[72,512]{1,0:T(8,128)} %get-tuple-element.30), channel_id=1, source_target_pairs={{0,32},{16,48},{32,64},{48,80},{64,96},{80,112},{1,33},{17,49},{33... | collective-permute-start | bytes 442376 | tf_op jit(solution)/shard_map/ppermute | solution.py:28
  357.4 30.7 %collective-permute-start.19 = (f32[72,512]{1,0:T(8,128)}, f32[72,512]{1,0:T(8,128)S(1)}, u32[]{:S(2)}, u32[]{:S(2)}) collective-permute-start(f32[72,512]{1,0:T(8,128)} %get-tuple-element.30), channel_id=1, source_target_pairs={{0,48},{16,64},{32,80},{48,96},{64,112},{1,49},{17,65},{33,81},{49... | collective-permute-start | bytes 442376 | tf_op jit(solution)/shard_map/ppermute | solution.py:28
  361.6 26.6 %collective-permute-start.20 = (f32[72,512]{1,0:T(8,128)}, f32[72,512]{1,0:T(8,128)S(1)}, u32[]{:S(2)}, u32[]{:S(2)}) collective-permute-start(f32[72,512]{1,0:T(8,128)} %get-tuple-element.30), channel_id=1, source_target_pairs={{0,64},{16,80},{32,96},{48,112},{1,65},{17,81},{33,97},{49,113},{2... | collective-permute-start | bytes 442376 | tf_op jit(solution)/shard_map/ppermute | solution.py:28
  364.1 24.1 %collective-permute-start.21 = (f32[72,512]{1,0:T(8,128)}, f32[72,512]{1,0:T(8,128)S(1)}, u32[]{:S(2)}, u32[]{:S(2)}) collective-permute-start(f32[72,512]{1,0:T(8,128)} %get-tuple-element.30), channel_id=1, source_target_pairs={{0,80},{16,96},{32,112},{1,81},{17,97},{33,113},{2,82},{18,98},{34... | collective-permute-start | bytes 442376 | tf_op jit(solution)/shard_map/ppermute | solution.py:28
  365.4 22.8 %collective-permute-start.22 = (f32[72,512]{1,0:T(8,128)}, f32[72,512]{1,0:T(8,128)S(1)}, u32[]{:S(2)}, u32[]{:S(2)}) collective-permute-start(f32[72,512]{1,0:T(8,128)} %get-tuple-element.30), channel_id=1, source_target_pairs={{0,96},{16,112},{1,97},{17,113},{2,98},{18,114},{3,99},{19,115},{4... | collective-permute-start | bytes 442376 | tf_op jit(solution)/shard_map/ppermute | solution.py:28
  367.4 19.4 %copy-start.14 = (f32[72,512]{1,0:T(8,128)S(1)}, f32[72,512]{1,0:T(8,128)}, u32[]{:S(2)}) copy-start(f32[72,512]{1,0:T(8,128)} %get-tuple-element.30) | copy-start | bytes 442372
  386.8 4.0 collective-permute-start.23
Sparse Core Ops, SparseCore 0:
  9.6 188.4 all-gather.5
  278.8 53.7 all-gather.3
